TPU v7x, 512 devices: a whole 4x4x16 slice. The times are simulated.
512 devices in a mesh: dp: 16 (over y, x_hi, core), ctx: 32 (over z, x_lo).
Axes of the slice: x: 4 (x_hi: 2, x_lo: 2; x = x_hi * 2 + x_lo), y: 4, z: 16, core: 2. Of those that a mesh axis runs over, the one named last changes fastest.
Arguments:
- queries: bfloat16 [16, 4096, 2048], P('dp', 'ctx'), may hold values from -64 to 64
- key_states: bfloat16 [16, 4096, 1024], P('dp', 'ctx'), may hold values from -6 to 6
- value_states: bfloat16 [16, 4096, 1024], P('dp', 'ctx'), may hold values from -6 to 6
- cotangent: bfloat16 [16, 4096, 5376], P('dp', 'ctx'), may hold values from -96 to 96
- core_aux: bfloat16 [16, 42, 8], replicated, may hold values from -0.5 to 0.5
- core_central: bfloat16 [8, 128, 128], replicated, may hold values from -0.5 to 0.5
Outputs:
- grad_queries: bfloat16 [16, 4096, 2048], P('dp', 'ctx')
- grad_keys: bfloat16 [16, 4096, 1024], P('dp', 'ctx')
- grad_values: bfloat16 [16, 4096, 1024], P('dp', 'ctx')
- grad_core: float32 [16, 42, 8], replicated
All inputs are finite; a program needn't handle non-finite values.
Results may differ from a plain program's by a relative error of at most 0.014.
The roundings to bfloat16 on the way count: a program that leaves them out, or rounds other values in their place, can miss the bound.
Values may be sent and summed in bfloat16 or wider, within the bound.
A program may use at most 128 MiB of HBM per device.

v0:
```python
import jax
import jax.numpy as jnp
from jax import lax
from jax.sharding import PartitionSpec as P

HD = 128
HQ = 16
HK = 8
J2 = 128
J1 = 42
BOND = 8
WINDOW = 1024


SCORE_SCALE = 168.0 ** (-0.5)
MASK_FILL = -1e30


def passed_along(x, axis, by):
    devices = lax.axis_size(axis)
    pairs = [(i, i + by) for i in range(devices) if 0 <= i + by < devices]
    return lax.ppermute(x, axis, pairs)


def attention_probs(query_heads, key_heads, first_pos, reach_blocks, tok_rows):
    extent = key_heads.shape[0]
    scores = (
        jnp.einsum("tkgd,rkd->kgtr", query_heads, key_heads, preferred_element_type=jnp.float32)
        * SCORE_SCALE
    )
    query_pos = first_pos + jnp.arange(tok_rows, dtype=jnp.int32)
    key_pos = first_pos - reach_blocks * tok_rows + jnp.arange(extent, dtype=jnp.int32)
    pos_gap = query_pos[:, None] - key_pos[None, :]
    allowed = (pos_gap >= 0) & (pos_gap < WINDOW) & (key_pos[None, :] >= 0)
    scores = jnp.where(allowed, scores, MASK_FILL)
    row_max = jnp.max(scores, axis=-1, keepdims=True)
    exp_terms = jnp.exp(scores - row_max)
    attn_prob = exp_terms / jnp.sum(exp_terms, axis=-1, keepdims=True)
    return (attn_prob, attn_prob.astype(jnp.bfloat16))


def core_terms(attn_part, cot_part, core_aux, core_central):
    sub_rows = attn_part.shape[0]
    hidden = lax.dot_general(
        cot_part.reshape(sub_rows * J1, J2),
        core_central.reshape(BOND * HD, J2),
        (((1,), (1,)), ((), ())),
        preferred_element_type=jnp.float32,
    )
    hidden = hidden.astype(jnp.bfloat16).reshape(sub_rows, J1, BOND, HD)
    attn_heads = attn_part.reshape(sub_rows, HQ, HD)
    grad_part = lax.dot_general(
        attn_heads, hidden, (((0, 2), (0, 3)), ((), ())), preferred_element_type=jnp.float32
    )
    d_attn = lax.dot_general(
        hidden, core_aux, (((1, 2), (1, 2)), ((), ())), preferred_element_type=jnp.float32
    )
    d_attn = jnp.swapaxes(d_attn, 1, 2).reshape(sub_rows, HQ * HD).astype(jnp.bfloat16)
    return (grad_part, d_attn)


def body(queries, key_states, value_states, cotangent, core_aux, core_central):
    query_rows = queries[0]
    key_rows = key_states[0]
    value_rows = value_states[0]
    cot_rows = cotangent[0]
    tok_rows = query_rows.shape[0]
    reach_blocks = WINDOW // tok_rows
    group_size = HQ // HK
    kv_width = HK * HD
    extent = (reach_blocks + 1) * tok_rows
    first_pos = lax.axis_index("ctx") * tok_rows
    parts_key = []
    parts_value = []
    for offset in range(reach_blocks, 0, -1):
        got_key, got_value = passed_along((key_rows, value_rows), "ctx", offset)
        parts_key.append(got_key)
        parts_value.append(got_value)
    window_key = jnp.concatenate(parts_key + [key_rows], 0)
    window_value = jnp.concatenate(parts_value + [value_rows], 0)
    query_heads = query_rows.reshape(tok_rows, HK, group_size, HD)
    key_heads = window_key.reshape(extent, HK, HD)
    value_heads = window_value.reshape(extent, HK, HD)
    attn_prob, prob_half = attention_probs(
        query_heads, key_heads, first_pos, reach_blocks, tok_rows
    )
    attn = jnp.einsum("kgtr,rkd->tkgd", prob_half, value_heads, preferred_element_type=jnp.float32)
    attn = attn.reshape(tok_rows, HQ * HD).astype(jnp.bfloat16)
    sub_rows = min(32, tok_rows)

    def core_step(core_acc, pair_rows):
        attn_part, cot_part = pair_rows
        grad_part, d_part = core_terms(attn_part, cot_part, core_aux, core_central)
        return (core_acc + grad_part, d_part)

    core_local, d_attn = lax.scan(
        core_step,
        jnp.zeros((HQ, J1, BOND), jnp.float32),
        (
            attn.reshape(tok_rows // sub_rows, sub_rows, HQ * HD),
            cot_rows.reshape(tok_rows // sub_rows, sub_rows, cot_rows.shape[1]),
        ),
    )
    d_attn = d_attn.reshape(tok_rows, HQ * HD)
    all_tokens = tok_rows * lax.axis_size("ctx") * lax.axis_size("dp")
    grad_core = lax.psum(core_local, ("dp", "ctx")) / jnp.sqrt(jnp.float32(all_tokens * HD))
    d_heads = d_attn.reshape(tok_rows, HK, group_size, HD)
    attn_group = attn.reshape(tok_rows, HK, group_size, HD)
    d_prob = jnp.einsum("tkgd,rkd->kgtr", d_heads, value_heads, preferred_element_type=jnp.float32)
    row_delta = jnp.sum(d_heads.astype(jnp.float32) * attn_group.astype(jnp.float32), axis=-1)
    row_delta = jnp.transpose(row_delta, (1, 2, 0))
    d_score = (attn_prob * (d_prob - row_delta[..., None])).astype(jnp.bfloat16)
    grad_query = (
        jnp.einsum("kgtr,rkd->tkgd", d_score, key_heads, preferred_element_type=jnp.float32)
        * SCORE_SCALE
    )
    grad_query = grad_query.reshape(tok_rows, HQ * HD).astype(jnp.bfloat16)
    key_terms = (
        jnp.einsum(
            "kgtr,tkgd->rkd", d_score, query_heads, preferred_element_type=jnp.float32
        ).reshape(extent, kv_width)
        * SCORE_SCALE
    )
    value_terms = jnp.einsum(
        "kgtr,tkgd->rkd", prob_half, d_heads, preferred_element_type=jnp.float32
    ).reshape(extent, kv_width)
    key_terms = key_terms.astype(jnp.bfloat16)
    value_terms = value_terms.astype(jnp.bfloat16)
    key_sum = key_terms[reach_blocks * tok_rows :].astype(jnp.float32)
    value_sum = value_terms[reach_blocks * tok_rows :].astype(jnp.float32)
    for offset in range(1, reach_blocks + 1):
        low_row = (reach_blocks - offset) * tok_rows
        got_key, got_value = passed_along(
            (key_terms[low_row : low_row + tok_rows], value_terms[low_row : low_row + tok_rows]),
            "ctx",
            -offset,
        )
        key_sum = key_sum + got_key.astype(jnp.float32)
        value_sum = value_sum + got_value.astype(jnp.float32)
    return (
        grad_query[None],
        key_sum.astype(jnp.bfloat16)[None],
        value_sum.astype(jnp.bfloat16)[None],
        grad_core,
    )


def solution(mesh):
    in_specs = (
        P("dp", "ctx", None),
        P("dp", "ctx", None),
        P("dp", "ctx", None),
        P("dp", "ctx", None),
        P(),
        P(),
    )
    out_specs = (P("dp", "ctx", None), P("dp", "ctx", None), P("dp", "ctx", None), P())
    return jax.shard_map(body, mesh=mesh, in_specs=in_specs, out_specs=out_specs, check_vma=False)
```

profile of v0, /device:TPU:6, one launch (start us, length us, event | category | flops | bytes accessed | tf_op | source)
XLA Modules:
  0.0 600.3 jit_solution(13661115022719675513)
XLA Ops:
  1.8 9.1 %collective-permute-start = (bf16[128,1024]{0,1:T(8,128)(2,1)S(1)}, bf16[128,1024]{0,1:T(8,128)(2,1)S(1)}, u32[]{:S(2)}, u32[]{:S(2)}) collective-permute-start(bf16[128,1024]{0,1:T(8,128)(2,1)S(1)} %bitcast.212), channel_id=1, source_target_pairs={{0,8},{1,9},{2,10},{3,11},{4,12},{5,13},{6,14},{7,15},{8,16},{9,17... | collective-permute-start | bytes 786440 | tf_op jit(solution)/shard_map/ppermute | solution.py:22
  10.9 9.4 %collective-permute-start.1 = (bf16[128,1024]{0,1:T(8,128)(2,1)S(1)}, bf16[128,1024]{0,1:T(8,128)(2,1)S(1)}, u32[]{:S(2)}, u32[]{:S(2)}) collective-permute-start(bf16[128,1024]{0,1:T(8,128)(2,1)S(1)} %bitcast.213), channel_id=1, source_target_pairs={{0,7},{1,8},{2,9},{3,10},{4,11},{5,12},{6,13},{7,14},{8,15},{9,16}... | collective-permute-start | bytes 786440 | tf_op jit(solution)/shard_map/ppermute | solution.py:22
  20.3 3.8 collective-permute-start.2
  24.1 4.0 collective-permute-start.3
  28.1 3.4 collective-permute-start.4
  31.6 7.7 %collective-permute-start.5 = (bf16[128,1024]{0,1:T(8,128)(2,1)S(1)}, bf16[128,1024]{0,1:T(8,128)(2,1)S(1)}, u32[]{:S(2)}, u32[]{:S(2)}) collective-permute-start(bf16[128,1024]{0,1:T(8,128)(2,1)S(1)} %bitcast.217), channel_id=1, source_target_pairs={{0,3},{1,4},{2,5},{3,6},{4,7},{5,8},{6,9},{7,10},{8,11},{9,12},{10... | collective-permute-start | bytes 786440 | tf_op jit(solution)/shard_map/ppermute | solution.py:22
  39.3 20.1 %collective-permute-start.6 = (bf16[128,1024]{0,1:T(8,128)(2,1)S(1)}, bf16[128,1024]{0,1:T(8,128)(2,1)S(1)}, u32[]{:S(2)}, u32[]{:S(2)}) collective-permute-start(bf16[128,1024]{0,1:T(8,128)(2,1)S(1)} %bitcast.218), channel_id=1, source_target_pairs={{0,2},{1,3},{2,4},{3,5},{4,6},{5,7},{6,8},{7,9},{8,10},{9,11},{10,... | collective-permute-start | bytes 786440 | tf_op jit(solution)/shard_map/ppermute | solution.py:22
  59.4 1.9 collective-permute-start.7
  61.3 1.5 fusion.42
  63.7 1.3 copy.126
  65.0 1.3 copy.75
  68.9 31.5 %collective-permute-start.8 = (bf16[128,1024]{1,0:T(8,128)(2,1)}, bf16[128,1024]{1,0:T(8,128)(2,1)}, u32[]{:S(2)}, u32[]{:S(2)}) collective-permute-start(bf16[128,1024]{1,0:T(8,128)(2,1)} %bitcast.14), channel_id=1, source_target_pairs={{0,8},{1,9},{2,10},{3,11},{4,12},{5,13},{6,14},{7,15},{8,16},{9,17... | collective-permute-start | bytes 786440 | tf_op jit(solution)/shard_map/ppermute | solution.py:22
  101.2 11.0 %collective-permute-start.9 = (bf16[128,1024]{1,0:T(8,128)(2,1)}, bf16[128,1024]{1,0:T(8,128)(2,1)}, u32[]{:S(2)}, u32[]{:S(2)}) collective-permute-start(bf16[128,1024]{1,0:T(8,128)(2,1)} %bitcast.14), channel_id=1, source_target_pairs={{0,7},{1,8},{2,9},{3,10},{4,11},{5,12},{6,13},{7,14},{8,15},{9,16}... | collective-permute-start | bytes 786440 | tf_op jit(solution)/shard_map/ppermute | solution.py:22
  113.1 33.2 %collective-permute-start.10 = (bf16[128,1024]{1,0:T(8,128)(2,1)}, bf16[128,1024]{1,0:T(8,128)(2,1)}, u32[]{:S(2)}, u32[]{:S(2)}) collective-permute-start(bf16[128,1024]{1,0:T(8,128)(2,1)} %bitcast.14), channel_id=1, source_target_pairs={{0,6},{1,7},{2,8},{3,9},{4,10},{5,11},{6,12},{7,13},{8,14},{9,15},... | collective-permute-start | bytes 786440 | tf_op jit(solution)/shard_map/ppermute | solution.py:22
  147.1 2.0 collective-permute-start.11
  151.0 7.6 %collective-permute-start.12 = (bf16[128,1024]{1,0:T(8,128)(2,1)}, bf16[128,1024]{1,0:T(8,128)(2,1)}, u32[]{:S(2)}, u32[]{:S(2)}) collective-permute-start(bf16[128,1024]{1,0:T(8,128)(2,1)} %bitcast.14), channel_id=1, source_target_pairs={{0,4},{1,5},{2,6},{3,7},{4,8},{5,9},{6,10},{7,11},{8,12},{9,13},{1... | collective-permute-start | bytes 786440 | tf_op jit(solution)/shard_map/ppermute | solution.py:22
  158.5 1.8 copy.64
  165.5 6.5 %fusion.55 = (f32[8,2,128]{2,1,0:T(2,128)S(1)}, f32[8,2,128,1152]{2,3,1,0:T(8,128)}) fusion(pred[128,1152]{0,1:T(8,128)(4,1)} %fusion.42, bf16[128,8,2,128]{0,3,2,1:T(8,128)(2,1)S(1)} %bitcast.192, bf16[1152,8,128]{2,0,1:T(8,128)(2,1)S(1)} %constant_dynamic-update-slice_fusion.1), kind=kOutput, calls=%fused_computation.77 | convolution fusion | flops 613418112 | bytes 12476416 | tf_op jit(solution)/shard_map/sub | solution.py:37
  172.1 7.1 %fusion.19 = bf16[8,2,128,1152]{2,3,1,0:T(8,128)(2,1)} fusion(f32[8,2,128,1152]{2,3,1,0:T(8,128)} %get-tuple-element.123, f32[8,2,128]{2,1,0:T(2,128)S(1)} %get-tuple-element.122), kind=kLoop, calls=%fused_computation.26 | loop fusion | flops 4718592 | bytes 14163968 | tf_op jit(solution)/shard_map/convert_element_type | solution.py:39
  179.1 10.6 %collective-permute-start.13 = (bf16[128,1024]{1,0:T(8,128)(2,1)}, bf16[128,1024]{1,0:T(8,128)(2,1)S(1)}, u32[]{:S(2)}, u32[]{:S(2)}) collective-permute-start(bf16[128,1024]{1,0:T(8,128)(2,1)} %bitcast.14), channel_id=1, source_target_pairs={{0,3},{1,4},{2,5},{3,6},{4,7},{5,8},{6,9},{7,10},{8,11},{9,12},{10... | collective-permute-start | bytes 786440 | tf_op jit(solution)/shard_map/ppermute | solution.py:22
  190.9 2.0 collective-permute-start.14
  194.1 2.6 collective-permute-start.15
  200.5 1.8 collective-permute-done.14
  203.6 3.1 collective-permute-done.15
  208.0 4.2 fusion.38
  213.3 2.2 convert_element_type.143
  215.5 33.2 %while.13 = (s32[]{:T(128)}, f32[16,42,8]{1,0,2:T(8,128)}, bf16[4,32,2048]{2,1,0:T(8,128)(2,1)}, bf16[4,32,2048]{2,1,0:T(8,128)(2,1)}, bf16[4,32,5376]{2,1,0:T(8...) while((s32[]{:T(128)}, f32[16,42,8]{1,0,2:T(8,128)}, ...), condition=%wide.region_3.4_spmd.clone, body=%wide.region_2.3_spmd.clone.sunk | while | flops 441854464 | bytes 17131632 | solution.py:96
  219.6 2.2 fusion.87
  227.2 3.1 fusion.87
  235.7 3.1 fusion.87
  244.2 3.1 fusion.87
  248.7 1.4 reshape_reshape.3
  250.7 3.9 fusion.21
  254.8 1.5 fusion.53
  256.3 1.9 copy.97
  258.2 1.9 collective-permute-start.24
  260.2 1.8 copy.99
  263.2 1.8 copy.100
  266.3 1.8 copy.101
  269.4 1.8 copy.102
  271.2 1.5 collective-permute-start.28
  272.7 1.8 copy.103
  274.5 4.9 fusion.13
  280.5 1.5 fusion.20
  282.0 1.4 collective-permute-start.29
  283.5 1.4 fusion.54
  289.3 1.3 collective-permute-start.30
  290.6 1.3 collective-permute-start.31
  291.9 21.4 %collective-permute-start.16 = (bf16[128,1024]{1,0:T(8,128)(2,1)}, bf16[128,1024]{1,0:T(8,128)(2,1)}, u32[]{:S(2)}, u32[]{:S(2)}) collective-permute-start(bf16[128,1024]{1,0:T(8,128)(2,1)} %copy.86), channel_id=1, source_target_pairs={{1,0},{2,1},{3,2},{4,3},{5,4},{6,5},{7,6},{8,7},{9,8},{10,9},{11,1... | collective-permute-start | bytes 786440 | tf_op jit(solution)/shard_map/ppermute | solution.py:22
  313.3 1.3 collective-permute-start.17
  314.6 29.2 %collective-permute-done.29 = bf16[128,1024]{1,0:T(8,128)(2,1)} collective-permute-done((bf16[128,1024]{1,0:T(8,128)(2,1)S(1)}, bf16[128,1024]{1,0:T(8,128)(2,1)}, u32[]{:S(2)}, u32[]{:S(2)}) %collective-permute-start.29) | collective-permute-done | bytes 262176 | tf_op jit(solution)/shard_map/ppermute | solution.py:22
  345.5 1.8 copy.90
  350.5 153.8 %psum.7 = f32[16,42,8]{1,2,0:T(8,128)S(1)} all-reduce(f32[16,42,8]{1,2,0:T(8,128)S(1)} %copy.106), channel_id=1, replica_groups=mesh['dp'=16,'ctx'=32] {'dp','ctx'}, use_global_device_ids=true, to_apply=%region_5.6 | all-reduce | flops 5376 | bytes 43008 | tf_op jit(solution)/shard_map/psum | solution.py:106
  505.0 1.3 collective-permute-start.19
  506.3 1.3 collective-permute-start.20
  507.6 1.3 collective-permute-start.21
  508.9 1.3 collective-permute-start.22
  510.2 1.3 collective-permute-start.23
  511.5 2.6 fusion.48
  514.1 5.5 collective-permute-done.19
  519.6 14.7 %collective-permute-done.20 = bf16[128,1024]{1,0:T(8,128)(2,1)S(1)} collective-permute-done((bf16[128,1024]{1,0:T(8,128)(2,1)S(1)}, bf16[128,1024]{1,0:T(8,128)(2,1)S(1)}, u32[]{:S(2)}, u32[]{:S(2)}) %collective-permute-start.20) | collective-permute-done | bytes 262176 | tf_op jit(solution)/shard_map/ppermute | solution.py:22
  534.3 16.4 %collective-permute-done.21 = bf16[128,1024]{1,0:T(8,128)(2,1)S(1)} collective-permute-done((bf16[128,1024]{1,0:T(8,128)(2,1)S(1)}, bf16[128,1024]{1,0:T(8,128)(2,1)S(1)}, u32[]{:S(2)}, u32[]{:S(2)}) %collective-permute-start.21) | collective-permute-done | bytes 262176 | tf_op jit(solution)/shard_map/ppermute | solution.py:22
  550.7 47.4 %collective-permute-done.22 = bf16[128,1024]{1,0:T(8,128)(2,1)S(1)} collective-permute-done((bf16[128,1024]{1,0:T(8,128)(2,1)S(1)}, bf16[128,1024]{1,0:T(8,128)(2,1)S(1)}, u32[]{:S(2)}, u32[]{:S(2)}) %collective-permute-start.22) | collective-permute-done | bytes 262176 | tf_op jit(solution)/shard_map/ppermute | solution.py:22
  598.1 2.2 fusion.47
  (166 shorter events, 60.7 us)
Async XLA Ops:
  0.6 65.7 %copy-start.17 = (bf16[16,42,8]{1,2,0:T(8,128)(2,1)S(1)}, bf16[16,42,8]{1,2,0:T(8,128)(2,1)}, u32[]{:S(2)}) copy-start(bf16[16,42,8]{1,2,0:T(8,128)(2,1)} %param.12) | copy-start | bytes 32260
  1.8 29.8 %collective-permute-start = (bf16[128,1024]{0,1:T(8,128)(2,1)S(1)}, bf16[128,1024]{0,1:T(8,128)(2,1)S(1)}, u32[]{:S(2)}, u32[]{:S(2)}) collective-permute-start(bf16[128,1024]{0,1:T(8,128)(2,1)S(1)} %bitcast.212), channel_id=1, source_target_pairs={{0,8},{1,9},{2,10},{3,11},{4,12},{5,13},{6,14},{7,15},{8,16},{9,17... | collective-permute-start | bytes 786440 | tf_op jit(solution)/shard_map/ppermute | solution.py:22
  10.9 28.4 %collective-permute-start.1 = (bf16[128,1024]{0,1:T(8,128)(2,1)S(1)}, bf16[128,1024]{0,1:T(8,128)(2,1)S(1)}, u32[]{:S(2)}, u32[]{:S(2)}) collective-permute-start(bf16[128,1024]{0,1:T(8,128)(2,1)S(1)} %bitcast.213), channel_id=1, source_target_pairs={{0,7},{1,8},{2,9},{3,10},{4,11},{5,12},{6,13},{7,14},{8,15},{9,16}... | collective-permute-start | bytes 786440 | tf_op jit(solution)/shard_map/ppermute | solution.py:22
  20.3 39.1 %collective-permute-start.2 = (bf16[128,1024]{0,1:T(8,128)(2,1)S(1)}, bf16[128,1024]{0,1:T(8,128)(2,1)S(1)}, u32[]{:S(2)}, u32[]{:S(2)}) collective-permute-start(bf16[128,1024]{0,1:T(8,128)(2,1)S(1)} %bitcast.214), channel_id=1, source_target_pairs={{0,6},{1,7},{2,8},{3,9},{4,10},{5,11},{6,12},{7,13},{8,14},{9,15},... | collective-permute-start | bytes 786440 | tf_op jit(solution)/shard_map/ppermute | solution.py:22
  24.1 44.8 %collective-permute-start.3 = (bf16[128,1024]{0,1:T(8,128)(2,1)S(1)}, bf16[128,1024]{0,1:T(8,128)(2,1)S(1)}, u32[]{:S(2)}, u32[]{:S(2)}) collective-permute-start(bf16[128,1024]{0,1:T(8,128)(2,1)S(1)} %bitcast.215), channel_id=1, source_target_pairs={{0,5},{1,6},{2,7},{3,8},{4,9},{5,10},{6,11},{7,12},{8,13},{9,14},{... | collective-permute-start | bytes 786440 | tf_op jit(solution)/shard_map/ppermute | solution.py:22
  28.1 73.0 %collective-permute-start.4 = (bf16[128,1024]{0,1:T(8,128)(2,1)S(1)}, bf16[128,1024]{0,1:T(8,128)(2,1)S(1)}, u32[]{:S(2)}, u32[]{:S(2)}) collective-permute-start(bf16[128,1024]{0,1:T(8,128)(2,1)S(1)} %bitcast.216), channel_id=1, source_target_pairs={{0,4},{1,5},{2,6},{3,7},{4,8},{5,9},{6,10},{7,11},{8,12},{9,13},{1... | collective-permute-start | bytes 786440 | tf_op jit(solution)/shard_map/ppermute | solution.py:22
  31.6 81.5 %collective-permute-start.5 = (bf16[128,1024]{0,1:T(8,128)(2,1)S(1)}, bf16[128,1024]{0,1:T(8,128)(2,1)S(1)}, u32[]{:S(2)}, u32[]{:S(2)}) collective-permute-start(bf16[128,1024]{0,1:T(8,128)(2,1)S(1)} %bitcast.217), channel_id=1, source_target_pairs={{0,3},{1,4},{2,5},{3,6},{4,7},{5,8},{6,9},{7,10},{8,11},{9,12},{10... | collective-permute-start | bytes 786440 | tf_op jit(solution)/shard_map/ppermute | solution.py:22
  39.3 107.8 %collective-permute-start.6 = (bf16[128,1024]{0,1:T(8,128)(2,1)S(1)}, bf16[128,1024]{0,1:T(8,128)(2,1)S(1)}, u32[]{:S(2)}, u32[]{:S(2)}) collective-permute-start(bf16[128,1024]{0,1:T(8,128)(2,1)S(1)} %bitcast.218), channel_id=1, source_target_pairs={{0,2},{1,3},{2,4},{3,5},{4,6},{5,7},{6,8},{7,9},{8,10},{9,11},{10,... | collective-permute-start | bytes 786440 | tf_op jit(solution)/shard_map/ppermute | solution.py:22
  59.4 91.5 %collective-permute-start.7 = (bf16[128,1024]{0,1:T(8,128)(2,1)S(1)}, bf16[128,1024]{0,1:T(8,128)(2,1)}, u32[]{:S(2)}, u32[]{:S(2)}) collective-permute-start(bf16[128,1024]{0,1:T(8,128)(2,1)S(1)} %bitcast.219), channel_id=1, source_target_pairs={{0,1},{1,2},{2,3},{3,4},{4,5},{5,6},{6,7},{7,8},{8,9},{9,10},{10,1... | collective-permute-start | bytes 786440 | tf_op jit(solution)/shard_map/ppermute | solution.py:22
  65.0 100.5 %copy-start.7 = (bf16[1,128,2048]{1,2,0:T(8,128)(2,1)}, bf16[1,128,2048]{1,2,0:T(8,128)(2,1)S(1)}, u32[]{:S(2)}) copy-start(bf16[1,128,2048]{1,2,0:T(8,128)(2,1)S(1)} %copy.126) | copy-start | bytes 1572868
  68.9 110.2 %collective-permute-start.8 = (bf16[128,1024]{1,0:T(8,128)(2,1)}, bf16[128,1024]{1,0:T(8,128)(2,1)}, u32[]{:S(2)}, u32[]{:S(2)}) collective-permute-start(bf16[128,1024]{1,0:T(8,128)(2,1)} %bitcast.14), channel_id=1, source_target_pairs={{0,8},{1,9},{2,10},{3,11},{4,12},{5,13},{6,14},{7,15},{8,16},{9,17... | collective-permute-start | bytes 786440 | tf_op jit(solution)/shard_map/ppermute | solution.py:22
  101.2 89.7 %collective-permute-start.9 = (bf16[128,1024]{1,0:T(8,128)(2,1)}, bf16[128,1024]{1,0:T(8,128)(2,1)}, u32[]{:S(2)}, u32[]{:S(2)}) collective-permute-start(bf16[128,1024]{1,0:T(8,128)(2,1)} %bitcast.14), channel_id=1, source_target_pairs={{0,7},{1,8},{2,9},{3,10},{4,11},{5,12},{6,13},{7,14},{8,15},{9,16}... | collective-permute-start | bytes 786440 | tf_op jit(solution)/shard_map/ppermute | solution.py:22
  113.1 81.0 %collective-permute-start.10 = (bf16[128,1024]{1,0:T(8,128)(2,1)}, bf16[128,1024]{1,0:T(8,128)(2,1)}, u32[]{:S(2)}, u32[]{:S(2)}) collective-permute-start(bf16[128,1024]{1,0:T(8,128)(2,1)} %bitcast.14), channel_id=1, source_target_pairs={{0,6},{1,7},{2,8},{3,9},{4,10},{5,11},{6,12},{7,13},{8,14},{9,15},... | collective-permute-start | bytes 786440 | tf_op jit(solution)/shard_map/ppermute | solution.py:22
  147.1 50.8 %collective-permute-start.11 = (bf16[128,1024]{1,0:T(8,128)(2,1)}, bf16[128,1024]{1,0:T(8,128)(2,1)}, u32[]{:S(2)}, u32[]{:S(2)}) collective-permute-start(bf16[128,1024]{1,0:T(8,128)(2,1)} %bitcast.14), channel_id=1, source_target_pairs={{0,5},{1,6},{2,7},{3,8},{4,9},{5,10},{6,11},{7,12},{8,13},{9,14},{... | collective-permute-start | bytes 786440 | tf_op jit(solution)/shard_map/ppermute | solution.py:22
  150.9 13.4 %copy-start.11 = (bf16[128,8,128]{2,0,1:T(8,128)(2,1)S(1)}, bf16[128,8,128]{2,0,1:T(8,128)(2,1)}, u32[]{:S(2)}) copy-start(bf16[128,8,128]{2,0,1:T(8,128)(2,1)} %copy.62) | copy-start | bytes 786436
  151.0 48.1 %collective-permute-start.12 = (bf16[128,1024]{1,0:T(8,128)(2,1)}, bf16[128,1024]{1,0:T(8,128)(2,1)}, u32[]{:S(2)}, u32[]{:S(2)}) collective-permute-start(bf16[128,1024]{1,0:T(8,128)(2,1)} %bitcast.14), channel_id=1, source_target_pairs={{0,4},{1,5},{2,6},{3,7},{4,8},{5,9},{6,10},{7,11},{8,12},{9,13},{1... | collective-permute-start | bytes 786440 | tf_op jit(solution)/shard_map/ppermute | solution.py:22
  160.3 4.1 copy-start.12
  160.3 4.1 copy-start.13
  165.5 6.6 %copy-start = (bf16[1152,8,128]{2,0,1:T(8,128)(2,1)}, bf16[1152,8,128]{2,0,1:T(8,128)(2,1)S(1)}, u32[]{:S(2)}) copy-start(bf16[1152,8,128]{2,0,1:T(8,128)(2,1)S(1)} %constant_dynamic-update-slice_fusion.1) | copy-start | bytes 7077892
  179.1 21.2 %collective-permute-start.13 = (bf16[128,1024]{1,0:T(8,128)(2,1)}, bf16[128,1024]{1,0:T(8,128)(2,1)S(1)}, u32[]{:S(2)}, u32[]{:S(2)}) collective-permute-start(bf16[128,1024]{1,0:T(8,128)(2,1)} %bitcast.14), channel_id=1, source_target_pairs={{0,3},{1,4},{2,5},{3,6},{4,7},{5,8},{6,9},{7,10},{8,11},{9,12},{10... | collective-permute-start | bytes 786440 | tf_op jit(solution)/shard_map/ppermute | solution.py:22
  190.9 11.4 %collective-permute-start.14 = (bf16[128,1024]{1,0:T(8,128)(2,1)}, bf16[128,1024]{1,0:T(8,128)(2,1)}, u32[]{:S(2)}, u32[]{:S(2)}) collective-permute-start(bf16[128,1024]{1,0:T(8,128)(2,1)} %bitcast.14), channel_id=1, source_target_pairs={{0,2},{1,3},{2,4},{3,5},{4,6},{5,7},{6,8},{7,9},{8,10},{9,11},{10,... | collective-permute-start | bytes 786440 | tf_op jit(solution)/shard_map/ppermute | solution.py:22
  194.1 12.6 %collective-permute-start.15 = (bf16[128,1024]{1,0:T(8,128)(2,1)}, bf16[128,1024]{1,0:T(8,128)(2,1)}, u32[]{:S(2)}, u32[]{:S(2)}) collective-permute-start(bf16[128,1024]{1,0:T(8,128)(2,1)} %bitcast.14), channel_id=1, source_target_pairs={{0,1},{1,2},{2,3},{3,4},{4,5},{5,6},{6,7},{7,8},{8,9},{9,10},{10,1... | collective-permute-start | bytes 786440 | tf_op jit(solution)/shard_map/ppermute | solution.py:22
  207.9 4.2 copy-start.5
  207.9 7.6 %copy-start.2 = (bf16[8,128,128]{2,1,0:T(8,128)(2,1)S(1)}, bf16[8,128,128]{2,1,0:T(8,128)(2,1)}, u32[]{:S(2)}) copy-start(bf16[8,128,128]{2,1,0:T(8,128)(2,1)} %param.13) | copy-start | bytes 786436
  212.2 3.4 copy-start.3
  250.7 3.9 copy-start.4
  256.3 18.2 %copy-start.6 = (bf16[1152,8,128]{0,2,1:T(8,128)(2,1)S(1)}, bf16[1152,8,128]{0,2,1:T(8,128)(2,1)}, u32[]{:S(2)}) copy-start(bf16[1152,8,128]{0,2,1:T(8,128)(2,1)} %copy-done.5) | copy-start | bytes 7077892
  258.2 23.8 %collective-permute-start.24 = (bf16[128,1024]{1,0:T(8,128)(2,1)}, bf16[128,1024]{1,0:T(8,128)(2,1)}, u32[]{:S(2)}, u32[]{:S(2)}) collective-permute-start(bf16[128,1024]{1,0:T(8,128)(2,1)} %copy.97), channel_id=1, source_target_pairs={{1,0},{2,1},{3,2},{4,3},{5,4},{6,5},{7,6},{8,7},{9,8},{10,9},{11,1... | collective-permute-start | bytes 786440 | tf_op jit(solution)/shard_map/ppermute | solution.py:22
  261.9 27.3 %collective-permute-start.25 = (bf16[128,1024]{1,0:T(8,128)(2,1)}, bf16[128,1024]{1,0:T(8,128)(2,1)}, u32[]{:S(2)}, u32[]{:S(2)}) collective-permute-start(bf16[128,1024]{1,0:T(8,128)(2,1)} %copy.99), channel_id=1, source_target_pairs={{2,0},{3,1},{4,2},{5,3},{6,4},{7,5},{8,6},{9,7},{10,8},{11,9},{12,... | collective-permute-start | bytes 786440 | tf_op jit(solution)/shard_map/ppermute | solution.py:22
  265.0 25.6 %collective-permute-start.26 = (bf16[128,1024]{1,0:T(8,128)(2,1)}, bf16[128,1024]{1,0:T(8,128)(2,1)}, u32[]{:S(2)}, u32[]{:S(2)}) collective-permute-start(bf16[128,1024]{1,0:T(8,128)(2,1)} %copy.100), channel_id=1, source_target_pairs={{3,0},{4,1},{5,2},{6,3},{7,4},{8,5},{9,6},{10,7},{11,8},{12,9},{13... | collective-permute-start | bytes 786440 | tf_op jit(solution)/shard_map/ppermute | solution.py:22
  268.1 23.8 %collective-permute-start.27 = (bf16[128,1024]{1,0:T(8,128)(2,1)}, bf16[128,1024]{1,0:T(8,128)(2,1)}, u32[]{:S(2)}, u32[]{:S(2)}) collective-permute-start(bf16[128,1024]{1,0:T(8,128)(2,1)} %copy.101), channel_id=1, source_target_pairs={{4,0},{5,1},{6,2},{7,3},{8,4},{9,5},{10,6},{11,7},{12,8},{13,9},{1... | collective-permute-start | bytes 786440 | tf_op jit(solution)/shard_map/ppermute | solution.py:22
  271.2 42.1 %collective-permute-start.28 = (bf16[128,1024]{1,0:T(8,128)(2,1)}, bf16[128,1024]{1,0:T(8,128)(2,1)}, u32[]{:S(2)}, u32[]{:S(2)}) collective-permute-start(bf16[128,1024]{1,0:T(8,128)(2,1)} %copy.102), channel_id=1, source_target_pairs={{5,0},{6,1},{7,2},{8,3},{9,4},{10,5},{11,6},{12,7},{13,8},{14,9},{... | collective-permute-start | bytes 786440 | tf_op jit(solution)/shard_map/ppermute | solution.py:22
  274.5 4.9 copy-start.1
  279.4 1.0 copy-start.8
  280.5 1.6 copy-start.14
  282.0 2.9 copy-start.9
  282.0 61.7 %collective-permute-start.29 = (bf16[128,1024]{1,0:T(8,128)(2,1)S(1)}, bf16[128,1024]{1,0:T(8,128)(2,1)}, u32[]{:S(2)}, u32[]{:S(2)}) collective-permute-start(bf16[128,1024]{1,0:T(8,128)(2,1)S(1)} %copy-done.14), channel_id=1, source_target_pairs={{6,0},{7,1},{8,2},{9,3},{10,4},{11,5},{12,6},{13,7},{14,8},{15,9},... | collective-permute-start | bytes 786440 | tf_op jit(solution)/shard_map/ppermute | solution.py:22
  288.3 59.0 %copy-start.10 = (bf16[128,8,128]{0,2,1:T(8,128)(2,1)S(1)}, bf16[128,8,128]{0,2,1:T(8,128)(2,1)}, u32[]{:S(2)}) copy-start(bf16[128,8,128]{0,2,1:T(8,128)(2,1)} %get-tuple-element.117) | copy-start | bytes 786436
  289.3 215.7 %collective-permute-start.30 = (bf16[128,1024]{1,0:T(8,128)(2,1)}, bf16[128,1024]{1,0:T(8,128)(2,1)}, u32[]{:S(2)}, u32[]{:S(2)}) collective-permute-start(bf16[128,1024]{1,0:T(8,128)(2,1)} %copy.104), channel_id=1, source_target_pairs={{7,0},{8,1},{9,2},{10,3},{11,4},{12,5},{13,6},{14,7},{15,8},{16,9}... | collective-permute-start | bytes 786440 | tf_op jit(solution)/shard_map/ppermute | solution.py:22
  290.6 215.7 %collective-permute-start.31 = (bf16[128,1024]{1,0:T(8,128)(2,1)}, bf16[128,1024]{1,0:T(8,128)(2,1)}, u32[]{:S(2)}, u32[]{:S(2)}) collective-permute-start(bf16[128,1024]{1,0:T(8,128)(2,1)} %copy.105), channel_id=1, source_target_pairs={{8,0},{9,1},{10,2},{11,3},{12,4},{13,5},{14,6},{15,7},{16,8},{17,9... | collective-permute-start | bytes 786440 | tf_op jit(solution)/shard_map/ppermute | solution.py:22
  291.9 215.7 %collective-permute-start.16 = (bf16[128,1024]{1,0:T(8,128)(2,1)}, bf16[128,1024]{1,0:T(8,128)(2,1)}, u32[]{:S(2)}, u32[]{:S(2)}) collective-permute-start(bf16[128,1024]{1,0:T(8,128)(2,1)} %copy.86), channel_id=1, source_target_pairs={{1,0},{2,1},{3,2},{4,3},{5,4},{6,5},{7,6},{8,7},{9,8},{10,9},{11,1... | collective-permute-start | bytes 786440 | tf_op jit(solution)/shard_map/ppermute | solution.py:22
  313.3 195.6 %collective-permute-start.17 = (bf16[128,1024]{1,0:T(8,128)(2,1)}, bf16[128,1024]{1,0:T(8,128)(2,1)}, u32[]{:S(2)}, u32[]{:S(2)}) collective-permute-start(bf16[128,1024]{1,0:T(8,128)(2,1)} %copy.88), channel_id=1, source_target_pairs={{2,0},{3,1},{4,2},{5,3},{6,4},{7,5},{8,6},{9,7},{10,8},{11,9},{12,... | collective-permute-start | bytes 786440 | tf_op jit(solution)/shard_map/ppermute | solution.py:22
  343.8 166.5 %collective-permute-start.18 = (bf16[128,1024]{1,0:T(8,128)(2,1)}, bf16[128,1024]{1,0:T(8,128)(2,1)}, u32[]{:S(2)}, u32[]{:S(2)}) collective-permute-start(bf16[128,1024]{1,0:T(8,128)(2,1)} %copy.89), channel_id=1, source_target_pairs={{3,0},{4,1},{5,2},{6,3},{7,4},{8,5},{9,6},{10,7},{11,8},{12,9},{13... | collective-permute-start | bytes 786440 | tf_op jit(solution)/shard_map/ppermute | solution.py:22
  348.2 158.1 %copy-start.15 = (bf16[128,1024]{1,0:T(8,128)(2,1)S(1)}, bf16[128,1024]{1,0:T(8,128)(2,1)}, u32[]{:S(2)}) copy-start(bf16[128,1024]{1,0:T(8,128)(2,1)} %copy.91) | copy-start | bytes 786436
  348.3 156.7 %copy-start.16 = (bf16[128,1024]{1,0:T(8,128)(2,1)S(1)}, bf16[128,1024]{1,0:T(8,128)(2,1)}, u32[]{:S(2)}) copy-start(bf16[128,1024]{1,0:T(8,128)(2,1)} %copy.90) | copy-start | bytes 786436
  505.0 14.6 %collective-permute-start.19 = (bf16[128,1024]{1,0:T(8,128)(2,1)S(1)}, bf16[128,1024]{1,0:T(8,128)(2,1)S(1)}, u32[]{:S(2)}, u32[]{:S(2)}) collective-permute-start(bf16[128,1024]{1,0:T(8,128)(2,1)S(1)} %copy-done.16), channel_id=1, source_target_pairs={{4,0},{5,1},{6,2},{7,3},{8,4},{9,5},{10,6},{11,7},{12,8},{13,9},{1... | collective-permute-start | bytes 786440 | tf_op jit(solution)/shard_map/ppermute | solution.py:22
  506.3 28.0 %collective-permute-start.20 = (bf16[128,1024]{1,0:T(8,128)(2,1)S(1)}, bf16[128,1024]{1,0:T(8,128)(2,1)S(1)}, u32[]{:S(2)}, u32[]{:S(2)}) collective-permute-start(bf16[128,1024]{1,0:T(8,128)(2,1)S(1)} %copy-done.15), channel_id=1, source_target_pairs={{5,0},{6,1},{7,2},{8,3},{9,4},{10,5},{11,6},{12,7},{13,8},{14,9},{... | collective-permute-start | bytes 786440 | tf_op jit(solution)/shard_map/ppermute | solution.py:22
  507.6 43.1 %collective-permute-start.21 = (bf16[128,1024]{1,0:T(8,128)(2,1)S(1)}, bf16[128,1024]{1,0:T(8,128)(2,1)S(1)}, u32[]{:S(2)}, u32[]{:S(2)}) collective-permute-start(bf16[128,1024]{1,0:T(8,128)(2,1)S(1)} %copy.92), channel_id=1, source_target_pairs={{6,0},{7,1},{8,2},{9,3},{10,4},{11,5},{12,6},{13,7},{14,8},{15,9},... | collective-permute-start | bytes 786440 | tf_op jit(solution)/shard_map/ppermute | solution.py:22
  508.9 89.2 %collective-permute-start.22 = (bf16[128,1024]{1,0:T(8,128)(2,1)S(1)}, bf16[128,1024]{1,0:T(8,128)(2,1)S(1)}, u32[]{:S(2)}, u32[]{:S(2)}) collective-permute-start(bf16[128,1024]{1,0:T(8,128)(2,1)S(1)} %copy.93), channel_id=1, source_target_pairs={{7,0},{8,1},{9,2},{10,3},{11,4},{12,5},{13,6},{14,7},{15,8},{16,9}... | collective-permute-start | bytes 786440 | tf_op jit(solution)/shard_map/ppermute | solution.py:22
  510.2 87.9 %collective-permute-start.23 = (bf16[128,1024]{1,0:T(8,128)(2,1)S(1)}, bf16[128,1024]{1,0:T(8,128)(2,1)S(1)}, u32[]{:S(2)}, u32[]{:S(2)}) collective-permute-start(bf16[128,1024]{1,0:T(8,128)(2,1)S(1)} %copy.94), channel_id=1, source_target_pairs={{8,0},{9,1},{10,2},{11,3},{12,4},{13,5},{14,6},{15,7},{16,8},{17,9... | collective-permute-start | bytes 786440 | tf_op jit(solution)/shard_map/ppermute | solution.py:22
where the time goes:
time: 608 us; the launch traced here: 600 us
  starting transfers between devices  201 us (33%)
  blocking collectives  154 us (25%)
  waiting for transfers between devices  118 us (19%)
  local copies, waits for them, and re-layouts  71.7 us (12%)
  matrix products  39.2 us (6%)
  other arithmetic  14.2 us (2%)
    ppermute x32, starting transfers between devices, passed_along(): return lax.ppermute(x, axis, pairs)  201 us
    psum x1, blocking collectives, body(): lax.psum(core_local, ('dp', 'ctx')) / jnp.sqrt(jnp.float32(all_tokens * HD))  154 us
    ppermute x32, waiting for transfers between devices, passed_along(): return lax.ppermute(x, axis, pairs)  118 us
    slice x9, local copies, waits for them, and re-layouts, body(): value_terms[low_row:low_row + tok_rows]  14.1 us
  transfers between devices with their start and end apart: 32, of which 7 were waited for; matrix products, arithmetic and copies ran while one was open for 12% of the time, Pallas kernels for 0%

commit v1 on v0

v1 whole, which is shorter than its diff:
```python
import functools
import math

import jax
import jax.numpy as jnp
from jax import lax
from jax.experimental import pallas as pl
from jax.experimental.pallas import tpu as pltpu
from jax.sharding import PartitionSpec as P

HD = 128
HQ = 16
HK = 8
J1 = 42
JP = 48
BOND = 8
WINDOW = 1024
TOK = 128
BLK = 2 * TOK
OWN = HK // 2
HOPS = WINDOW // BLK
COLS = 2 * BLK
SCORE_SCALE = 168.0 ** (-0.5)
EXP_SCALE = SCORE_SCALE * math.log2(math.e)
MASK_FILL = -1e30
F32 = jnp.float32
BF16 = jnp.bfloat16
MESH = pl.DeviceIdType.MESH


def reduce_stages(mesh_shape):
    stages = []
    for axis in ("dp", "ctx"):
        bits = mesh_shape[axis].bit_length() - 1
        shift = 0
        while bits > 0:
            take = min(2, bits)
            stages.append((axis, shift, 1 << take))
            shift += take
            bits -= take
    return stages


def nt(a, b):
    return lax.dot_general(a, b, (((1,), (1,)), ((), ())), preferred_element_type=F32)


def nn(a, b):
    return lax.dot_general(a, b, (((1,), (0,)), ((), ())), preferred_element_type=F32)


def lanes(start):
    return pl.ds(pl.multiple_of(start * HD, HD), HD)


def rows(start):
    return pl.ds(pl.multiple_of(start * TOK, TOK), TOK)


def kernel(
    n_ctx, stages,
    q_ref, k_ref, v_ref, cot_ref, aux_ref, cen_ref,
    dq_ref, dk_ref, dv_ref, core_ref,
    kv, qbuf, dabuf, dasend, atx, atin, dqx, csend, crecv, finx, arbuf,
    cots, est, mat, cent, kt, vt, dat, sc, ph, ds, part,
    kx_s, kx_r, loc, qx_s, qx_r, qloc, hop_s, hop_r, da_s, da_r, at_s, at_r,
    dq_s, dq_r, ch_s, ch_r, fin_s, fin_r, ar_s, ar_r,
):
    me_dp = lax.axis_index("dp")
    me = lax.axis_index("ctx")
    zpos = me // 2
    xlo = lax.rem(me, 2)
    other = 1 - xlo
    partner = {"ctx": me + 1 - 2 * xlo}
    up = {"ctx": lax.rem(me + 2, n_ctx)}
    down = {"ctx": lax.rem(me + n_ctx - 2, n_ctx)}
    at_axis = {"dp": me_dp, "ctx": me}

    def stage_peers(stage):
        axis, shift, size = stage
        here = at_axis[axis]
        pos = lax.rem(here // (1 << shift), size)
        out = []
        for d in range(1, size):
            their = lax.rem(pos + d, size)
            out.append((d, {axis: here + (their - pos) * (1 << shift)}))
        return pos, out

    def remote(src, dst, s, r, dev):
        return pltpu.make_async_remote_copy(
            src_ref=src, dst_ref=dst, send_sem=s, recv_sem=r, device_id=dev, device_id_type=MESH
        )

    barrier = pltpu.get_barrier_semaphore()
    greet = [partner, up, down]
    for stage in stages:
        greet += [dev for _, dev in stage_peers(stage)[1]]
    for dev in greet:
        pl.semaphore_signal(barrier, inc=1, device_id=dev, device_id_type=MESH)
    pl.semaphore_wait(barrier, len(greet))

    srcs = (k_ref, v_ref)

    def kx(h, c):
        return remote(
            srcs[c].at[:, lanes(other * OWN + h)], kv.at[0, h, c, rows(xlo)],
            kx_s.at[h, c], kx_r.at[h, c], partner,
        )

    def kloc(h, c):
        return pltpu.make_async_copy(
            srcs[c].at[:, lanes(xlo * OWN + h)], kv.at[0, h, c, rows(xlo)], loc.at[h, c]
        )

    def qx(h, g):
        return remote(
            q_ref.at[:, lanes(other * 2 * OWN + 2 * h + g)], qbuf.at[h, rows(2 * g + xlo)],
            qx_s.at[h, g], qx_r.at[h, g], partner,
        )

    def qlocal(h, g):
        return pltpu.make_async_copy(
            q_ref.at[:, lanes(xlo * 2 * OWN + 2 * h + g)], qbuf.at[h, rows(2 * g + xlo)], qloc.at[h, g]
        )

    def hop(s, h):
        return remote(kv.at[s - 1, h], kv.at[s, h], hop_s.at[s - 1, h], hop_r.at[s - 1, h], up)

    def dax(h, g):
        return remote(
            dasend.at[h, g], dabuf.at[h, rows(2 * g + xlo)], da_s.at[h, g], da_r.at[h, g], partner
        )

    def attnx(h, g):
        return remote(
            atx.at[h, rows(2 * g + other)], atin.at[h, g], at_s.at[h, g], at_r.at[h, g], partner
        )

    def dqxc(h, g):
        return remote(
            dqx.at[h, rows(2 * g + other)], dq_ref.at[:, lanes(xlo * 2 * OWN + 2 * h + g)],
            dq_s.at[h, g], dq_r.at[h, g], partner,
        )

    def chain(st, h):
        return remote(csend.at[st, h], crecv.at[st, h], ch_s.at[st, h], ch_r.at[st, h], down)

    outs = (dk_ref, dv_ref)

    def finc(h, c):
        return remote(
            finx.at[h, c], outs[c].at[:, lanes(xlo * OWN + h)], fin_s.at[h, c], fin_r.at[h, c], partner
        )

    for h in range(OWN):
        for c in range(2):
            kx(h, c).start()
            kloc(h, c).start()
    for h in range(OWN):
        for c in range(2):
            qx(h, c).start()
            qlocal(h, c).start()

    for t_pad in range(1):
        @pl.loop(0, TOK)
        def _(t):
            cots[pl.ds(t * JP + JP - 8, 8), :] = jnp.zeros((8, HD), F32)

    @pl.loop(0, J1)
    def _(j):
        cots[pl.ds(j, TOK, stride=JP), :] = cot_ref[:, lanes(j)].astype(F32)

    @pl.loop(0, BOND)
    def _(b):
        cent[rows(b), :] = cen_ref[b].T

    def cot_tok(t):
        return cots[pl.ds(pl.multiple_of(t * JP, JP), JP), :].astype(BF16)

    def e_terms(t):
        e = nn(aux_ref[...], cot_tok(t)).astype(BF16)
        r16 = pl.ds(pl.multiple_of(t * HQ, HQ), HQ)
        for b in range(BOND):
            est[r16, b * HD : (b + 1) * HD] = e[b * HQ : (b + 1) * HQ]

    order = sorted(((s, h) for s in range(1, HOPS + 1) for h in range(OWN)), key=lambda a: (a[0] + a[1], -a[0]))
    per = TOK // len(order)
    for n, (s, h) in enumerate(order):
        if s == 1:
            for c in range(2):
                kx(h, c).wait_recv()
                kloc(h, c).wait()
        else:
            hop(s - 1, h).wait_recv()
        hop(s, h).start()

        @pl.loop(n * per, (n + 1) * per, unroll=4)
        def _(t):
            e_terms(t)

    @pl.loop(0, 8)
    def _(n):
        rr = pl.ds(pl.multiple_of(n * 256, 256), 256)
        mat[rr, :] = nn(est[rr, :], cent[...]).astype(BF16).astype(F32)

    for h in range(OWN):
        for g in range(2):
            i_other = other * 2 * OWN + 2 * h + g
            dasend[h, g] = mat[pl.ds(i_other, TOK, stride=HQ), :].astype(BF16)
    for h in range(OWN):
        for g in range(2):
            dax(h, g).start()
    for h in range(OWN):
        for g in range(2):
            i_own = xlo * 2 * OWN + 2 * h + g
            dabuf[h, rows(2 * g + xlo)] = mat[pl.ds(i_own, TOK, stride=HQ), :].astype(BF16)

    for h in range(OWN):
        for g in range(2):
            qx(h, g).wait_recv()
            qlocal(h, g).wait()
            dax(h, g).wait_recv()

    t_pos = lax.rem(lax.broadcasted_iota(jnp.int32, (TOK, COLS), 1), BLK)
    r_iota = lax.broadcasted_iota(jnp.int32, (TOK, COLS), 0)

    def service(n):
        for st in range(HOPS + 1):
            hh = n - st

            @pl.when(jnp.logical_and(hh >= 0, hh < OWN))
            def _():
                if st == 0:
                    total = part[hh, HOPS]
                else:
                    chain(st - 1, hh).wait_recv()
                    total = crecv[st - 1, hh].astype(F32) + part[hh, HOPS - st]
                total = total.astype(BF16)
                if st < HOPS:
                    csend[st, hh] = total
                    chain(st, hh).start()
                else:
                    part[hh, 0] = total.astype(F32)
                    for c in range(2):
                        finx[hh, c] = part[hh, 0, c, rows(other)].astype(BF16)
                        finc(hh, c).start()
                        outs[c][:, lanes(xlo * OWN + hh)] = part[hh, 0, c, rows(xlo)].astype(BF16)

    @pl.loop(0, OWN)
    def _(h):
        hop(HOPS, h).wait_recv()
        qh = qbuf[h]
        dah = dabuf[h]
        dat[...] = dah.T
        for s in range(HOPS + 1):
            for u in range(2):
                w = 2 * s + u
                kt[:, w * TOK : (w + 1) * TOK] = kv[s, h, 0, u * TOK : (u + 1) * TOK].T
                vt[:, w * TOK : (w + 1) * TOK] = kv[s, h, 1, u * TOK : (u + 1) * TOK].T

        def scores(s, u):
            return nt(kv[s, h, 0, rows(u)], qh)

        m = jnp.full((1, COLS), MASK_FILL, F32)
        for u in range(2):
            causal = t_pos >= r_iota + u * TOK
            far = jnp.where(zpos >= HOPS, scores(HOPS, u), MASK_FILL)
            x = jnp.where(causal, scores(0, u), far)
            sc[u * TOK : (u + 1) * TOK, :] = x
            m = jnp.maximum(m, jnp.max(x, axis=0, keepdims=True))

        def score_step(w, m):
            s = w // 2
            x = jnp.where(zpos >= s, scores(s, lax.rem(w, 2)), MASK_FILL)
            sc[rows(w), :] = x
            return jnp.maximum(m, jnp.max(x, axis=0, keepdims=True))

        m = lax.fori_loop(2, 2 * HOPS, score_step, m)

        def exp_step(w, l):
            e = jnp.exp2((sc[rows(w), :] - m) * EXP_SCALE)
            sc[rows(w), :] = e
            return l + jnp.sum(e, axis=0, keepdims=True)

        l = lax.fori_loop(0, 2 * HOPS, exp_step, jnp.zeros((1, COLS), F32))
        inv = 1.0 / l

        for u in range(2):
            causal = t_pos >= r_iota + u * TOK
            p = sc[u * TOK : (u + 1) * TOK, :] * inv
            sc[u * TOK : (u + 1) * TOK, :] = p
            ph[u * TOK : (u + 1) * TOK, :] = jnp.where(causal, p, 0.0).astype(BF16)
            w = 2 * HOPS + u
            ph[w * TOK : (w + 1) * TOK, :] = jnp.where(causal, 0.0, p).astype(BF16)

        @pl.loop(2, 2 * HOPS)
        def _(w):
            p = sc[rows(w), :] * inv
            sc[rows(w), :] = p
            ph[rows(w), :] = p.astype(BF16)

        att = nn(vt[...], ph[...]).astype(BF16)
        delta = jnp.sum(att.astype(F32) * dat[...].astype(F32), axis=0, keepdims=True)
        atx[h] = att.T
        for g in range(2):
            attnx(h, g).start()

        def dprob(s, u):
            return nn(kv[s, h, 1, rows(u)], dat[...])

        for u in range(2):
            causal = t_pos >= r_iota + u * TOK
            dp = jnp.where(causal, dprob(0, u), dprob(HOPS, u))
            d = sc[u * TOK : (u + 1) * TOK, :] * (dp - delta)
            ds[u * TOK : (u + 1) * TOK, :] = jnp.where(causal, d, 0.0).astype(BF16)
            w = 2 * HOPS + u
            ds[w * TOK : (w + 1) * TOK, :] = jnp.where(causal, 0.0, d).astype(BF16)

        @pl.loop(2, 2 * HOPS)
        def _(w):
            dp = dprob(w // 2, lax.rem(w, 2))
            ds[rows(w), :] = (sc[rows(w), :] * (dp - delta)).astype(BF16)

        dqt = (nn(kt[...], ds[...]) * SCORE_SCALE).astype(BF16)
        dqx[h] = dqt.T
        for g in range(2):
            dqxc(h, g).start()
        for g in range(2):
            dq_ref[:, lanes(xlo * 2 * OWN + 2 * h + g)] = dqx[h, rows(2 * g + xlo)]

        @pl.loop(0, HOPS + 1)
        def _(s):
            for u in range(2):
                rr = rows(2 * s + u)
                part[h, s, 0, u * TOK : (u + 1) * TOK] = nn(ds[rr, :], qh) * SCORE_SCALE
                part[h, s, 1, u * TOK : (u + 1) * TOK] = nn(ph[rr, :], dah)

        service(h)

    service(OWN)

    for h in range(OWN):
        for g in range(2):
            i_own = xlo * 2 * OWN + 2 * h + g
            mat[pl.ds(i_own, TOK, stride=HQ), :] = atx[h, rows(2 * g + xlo)].astype(F32)
    for h in range(OWN):
        for g in range(2):
            attnx(h, g).wait_recv()
            i_other = other * 2 * OWN + 2 * h + g
            mat[pl.ds(i_other, TOK, stride=HQ), :] = atin[h, g].astype(F32)

    @pl.loop(0, 8)
    def _(n):
        rr = pl.ds(pl.multiple_of(n * 256, 256), 256)
        a = mat[rr, :].astype(BF16)
        for b in range(BOND):
            est[rr, b * HD : (b + 1) * HD] = nn(a, cen_ref[b]).astype(BF16)

    service(OWN + 1)

    def core_step(t, acc):
        r16 = pl.ds(pl.multiple_of(t * HQ, HQ), HQ)
        f = jnp.concatenate([est[r16, b * HD : (b + 1) * HD] for b in range(BOND)], axis=0)
        return acc + nt(cot_tok(t), f)

    core_ref[...] = lax.fori_loop(0, TOK, core_step, jnp.zeros((JP, BOND * HQ), F32), unroll=4)

    for k, stage in enumerate(stages):
        pos, peers = stage_peers(stage)
        arbuf[k, pos] = core_ref[...]

        def copy(d, dev):
            return remote(arbuf.at[k, pos], arbuf.at[k, pos], ar_s.at[k, d], ar_r.at[k, d], dev)

        for d, dev in peers:
            copy(d, dev).start()
        if k < OWN - 2:
            service(OWN + 2 + k)
        for d, dev in peers:
            copy(d, dev).wait_recv()
        total = arbuf[k, 0]
        for n in range(1, stage[2]):
            total = total + arbuf[k, n]
        core_ref[...] = total
        for d, dev in peers:
            copy(d, dev).wait_send()
    for k in range(max(0, min(OWN - 2, len(stages))), OWN - 2):
        service(OWN + 2 + k)

    for h in range(OWN):
        for c in range(2):
            kx(h, c).wait_send()
            qx(h, c).wait_send()
            dax(h, c).wait_send()
            attnx(h, c).wait_send()
            dqxc(h, c).wait()
            finc(h, c).wait()
        for s in range(HOPS):
            hop(s + 1, h).wait_send()
            chain(s, h).wait_send()


def solution(mesh):
    n_ctx = mesh.shape["ctx"]
    stages = reduce_stages(mesh.shape)
    all_tokens = TOK * n_ctx * mesh.shape["dp"]

    def step(queries, key_states, value_states, cotangent, core_aux, core_central):
        aux = jnp.transpose(core_aux, (2, 0, 1)).reshape(BOND * HQ, J1)
        aux = jnp.pad(aux, ((0, 0), (0, JP - J1)))
        vm = pl.BlockSpec(memory_space=pltpu.VMEM)
        dma = pltpu.SemaphoreType.DMA
        pair = dma((OWN, 2))
        width = 2 * OWN * HD
        most = max(size for _, _, size in stages)
        dq, dk, dv, core = pl.pallas_call(
            functools.partial(kernel, n_ctx, stages),
            out_shape=(
                jax.ShapeDtypeStruct((TOK, HQ * HD), BF16),
                jax.ShapeDtypeStruct((TOK, HK * HD), BF16),
                jax.ShapeDtypeStruct((TOK, HK * HD), BF16),
                jax.ShapeDtypeStruct((JP, BOND * HQ), F32),
            ),
            in_specs=[vm] * 6,
            out_specs=(vm, vm, vm, vm),
            scratch_shapes=[
                pltpu.VMEM((HOPS + 1, OWN, 2, BLK, HD), BF16),
                pltpu.VMEM((OWN, COLS, HD), BF16),
                pltpu.VMEM((OWN, COLS, HD), BF16),
                pltpu.VMEM((OWN, 2, TOK, HD), BF16),
                pltpu.VMEM((OWN, COLS, HD), BF16),
                pltpu.VMEM((OWN, 2, TOK, HD), BF16),
                pltpu.VMEM((OWN, COLS, HD), BF16),
                pltpu.VMEM((HOPS, OWN, 2, BLK, HD), BF16),
                pltpu.VMEM((HOPS, OWN, 2, BLK, HD), BF16),
                pltpu.VMEM((OWN, 2, TOK, HD), BF16),
                pltpu.VMEM((len(stages), most, JP, BOND * HQ), F32),
                pltpu.VMEM((TOK * JP, HD), F32),
                pltpu.VMEM((TOK * HQ, BOND * HD), BF16),
                pltpu.VMEM((TOK * HQ, HD), F32),
                pltpu.VMEM((BOND * HD, HD), BF16),
                pltpu.VMEM((HD, (HOPS + 1) * BLK), BF16),
                pltpu.VMEM((HD, (HOPS + 1) * BLK), BF16),
                pltpu.VMEM((HD, COLS), BF16),
                pltpu.VMEM((HOPS * BLK, COLS), F32),
                pltpu.VMEM(((HOPS + 1) * BLK, COLS), BF16),
                pltpu.VMEM(((HOPS + 1) * BLK, COLS), BF16),
                pltpu.VMEM((OWN, HOPS + 1, 2, BLK, HD), F32),
                pair, pair, pair, pair, pair, pair,
                dma((HOPS, OWN)), dma((HOPS, OWN)),
                pair, pair, pair, pair, pair, pair,
                dma((HOPS, OWN)), dma((HOPS, OWN)),
                pair, pair,
                dma((len(stages), most)), dma((len(stages), most)),
            ],
            compiler_params=pltpu.CompilerParams(
                collective_id=0, has_side_effects=True, vmem_limit_bytes=60 * 1024 * 1024
            ),
        )(queries[0], key_states[0], value_states[0], cotangent[0], aux, core_central)
        core = jnp.transpose(core[:J1].reshape(J1, BOND, HQ), (2, 0, 1))
        core = core / jnp.sqrt(jnp.float32(all_tokens * HD))
        return dq[None], dk[None], dv[None], core

    return jax.shard_map(
        step,
        mesh=mesh,
        in_specs=(P("dp", "ctx", None),) * 4 + (P(), P()),
        out_specs=(P("dp", "ctx", None),) * 3 + (P(),),
        check_vma=False,
    )
```

time: 608 us -> 164 us (0.27); the launches traced: 600 us -> 163 us
  starting transfers between devices: 201 us -> 0 us
  Pallas kernels: 0 us -> 156 us
  blocking collectives: 154 us -> 0 us
  waiting for transfers between devices: 118 us -> 0 us
  local copies, waits for them, and re-layouts: 71.7 us -> 5.44 us
  matrix products: 39.2 us -> 0 us
  other arithmetic: 14.2 us -> 0.8 us
    ppermute x32 -> x0, starting transfers between devices: 201 us -> none  [passed_along(): return lax.ppermute(x, axis, pairs)]
    pallas_call x0 -> x1, Pallas kernels: none -> 156 us  [step(): pl.pallas_call(functools.partial(kernel, n_ctx, stages), out_shape=(jax.S...]
    psum x1 -> x0, blocking collectives: 154 us -> none  [body(): lax.psum(core_local, ('dp', 'ctx')) / jnp.sqrt(jnp.float32(all_tokens * HD))]
    ppermute x32 -> x0, waiting for transfers between devices: 118 us -> none  [passed_along(): return lax.ppermute(x, axis, pairs)]
    dot_general x17 -> x0, matrix products: 32.6 us -> none  [the longest x4 11.5 us: core_terms(): lax.dot_general(attn_heads, hidden, (((0, 2), (0, 3)), ((), ())), preferr...]
    slice x18 -> x0, local copies, waits for them, and re-layouts: 21.2 us -> none  [the longest x9 14.1 us: body(): value_terms[low_row:low_row + tok_rows]]
    concatenate x11 -> x0, local copies, waits for them, and re-layouts: 9.62 us -> none  [the longest x10 9.56 us: body(): window_key = jnp.concatenate(parts_key + [key_rows], 0)]
    while x17 -> x0, local copies, waits for them, and re-layouts: 8.07 us -> none
  transfers between devices with their start and end apart: 32 -> 0, of which waited for: 7 -> 0; matrix products, arithmetic and copies ran while one was open for 12% -> 0% of each run, Pallas kernels for 0% -> 0%
where the time goes in v1:
time: 164 us; the launch traced here: 163 us
  Pallas kernels  156 us (95%)
  local copies, waits for them, and re-layouts  5.44 us (3%)
    pallas_call x1, Pallas kernels, step(): pl.pallas_call(functools.partial(kernel, n_ctx, stages), out_shape=(jax.S...  156 us
    unnamed x8, local copies, waits for them, and re-layouts  3.95 us

profile of v1, /device:TPU:6, one launch (start us, length us, event | category | flops | bytes accessed | tf_op | source)
XLA Modules:
  0.0 162.9 jit_solution(9722208477612033877)
XLA Ops:
  0.6 0.8 copy.12
  1.4 0.6 pad.4.aux_ref
  2.0 156.0 %shard_map.93 = (bf16[128,2048]{1,0:T(8,128)(2,1)}, bf16[128,1024]{1,0:T(8,128)(2,1)}, bf16[128,1024]{1,0:T(8,128)(2,1)}, f32[48,128]{1,0:T(8,128)}) custom-call(bf16[128,2048]{1,0:T(8,128)(2,1)} %bitcast.14, bf16[128,1024]{1,0:T(8,128)(2,1)} %bitcast.18, bf16[128,1024]{1,0:T(8,128)(2,1)} %bitcast.19, bf16[128,5376]{1,0:T(8,128)(2,1)} %bitcast.12, ...), custom_call_target="tpu_custom_call" | custom-call | tf_op jit(solution)/shard_map/pallas_call | solution.py:416
  158.0 0.0 copy-start.1
  158.0 0.0 copy-start
  158.0 0.8 slice_multiply_fusion
  158.8 0.1 copy.13
  158.9 0.7 copy.14
  159.6 1.9 %copy.18 = bf16[1,128,2048]{2,1,0:T(8,128)(2,1)} copy(bf16[1,128,2048]{2,1,0:T(8,128)(2,1)} %bitcast.13) | data formatting | bytes 1048576
  161.5 0.0 copy-done.1
  161.5 0.7 copy.19
  162.2 0.0 copy-done
  162.2 0.7 copy.20
Async XLA Ops:
  158.0 3.5 %copy-start.1 = (bf16[128,1024]{1,0:T(8,128)(2,1)S(1)}, bf16[128,1024]{1,0:T(8,128)(2,1)}, u32[]{:S(2)}) copy-start(bf16[128,1024]{1,0:T(8,128)(2,1)} %get-tuple-element.9) | copy-start | bytes 786436
  158.0 4.2 %copy-start = (bf16[128,1024]{1,0:T(8,128)(2,1)S(1)}, bf16[128,1024]{1,0:T(8,128)(2,1)}, u32[]{:S(2)}) copy-start(bf16[128,1024]{1,0:T(8,128)(2,1)} %get-tuple-element.10) | copy-start | bytes 786436

commit v2 on v1

--- a/solution.py
+++ b/solution.py
@@ -27,18 +27,50 @@
 BF16 = jnp.bfloat16
 MESH = pl.DeviceIdType.MESH
 
+FIRST = [
+    "e", "e", "e", "e", ("f", 1, 0, 0), "e", "e", "e", ("f", 1, 0, 1), "e", "e", "e", ("f", 1, 1, 0), "e",
+    "e", "e", "e", ("f", 2, 0, 0), "e", "e", "d", ("f", 2, 0, 1), ("f", 1, 1, 1), ("f", 3, 0, 0),
+    ("f", 3, 0, 1), ("f", 2, 1, 0), ("f", 4, 0, 0), ("f", 4, 0, 1), ("f", 2, 1, 1), ("f", 3, 1, 0),
+]
+HOOKS = {
+    (0, "b"): [("f", 1, 2, 0)],
+    (0, "e"): [("f", 3, 1, 1)],
+    (0, "f"): [("b", 0, 0, 1)],
+    (0, "g"): [("f", 4, 1, 0)],
+    (0, "h"): [("f", 1, 2, 1), ("b", 0, 0, 0), ("f", 4, 1, 1), ("b", 1, 0, 1), ("f", 2, 2, 0)],
+    (1, "b"): [("b", 1, 0, 0), ("f", 2, 2, 1)],
+    (1, "c"): [("f", 1, 3, 0)],
+    (1, "d"): [("b", 2, 0, 1)],
+    (1, "f"): [("f", 3, 2, 0)],
+    (1, "g"): [("b", 0, 1, 1), ("f", 3, 2, 1)],
+    (1, "h"): [("b", 0, 1, 0), ("f", 1, 3, 1), ("b", 2, 0, 0), ("f", 4, 2, 0), ("b", 1, 1, 1), ("f", 4, 2, 1), ("b", 1, 1, 0), ("f", 2, 3, 0), ("b", 3, 0, 1), ("f", 2, 3, 1)],
+    (2, "b"): [("b", 2, 1, 1)],
+    (2, "d"): [("b", 2, 1, 0)],
+    (2, "e"): [("f", 3, 3, 0)],
+    (2, "g"): [("f", 3, 3, 1), ("b", 0, 2, 1), ("b", 3, 0, 0), ("b", 4, 0, 1)],
+    (2, "h"): [("f", 4, 3, 0), ("b", 0, 2, 0), ("f", 4, 3, 1), ("b", 1, 2, 1), ("b", 3, 1, 1), ("b", 3, 1, 0), ("b", 4, 0, 0)],
+    (3, "c"): [("b", 1, 2, 0)],
+    (3, "f"): [("b", 0, 3, 1), ("b", 2, 2, 1), ("b", 4, 1, 1)],
+    (3, "g"): [("b", 4, 1, 0)],
+}
+LAST = [
+    "f", ("b", 0, 3, 0), "f", "f", ("b", 1, 3, 1), "f", "g", ("b", 2, 2, 0), "g", "g", ("b", 1, 3, 0), "g",
+    "g", ("b", 2, 3, 1), "g", "g", ("b", 3, 2, 1), "g", ("a", 0), ("b", 2, 3, 0), ("b", 3, 2, 0), ("a", 1),
+    ("b", 3, 3, 1), ("b", 4, 2, 1), ("b", 3, 3, 0), ("b", 4, 2, 0), ("a", 2), ("b", 4, 3, 1), ("b", 4, 3, 0),
+    ("a", 3),
+]
+
 
 def reduce_stages(mesh_shape):
-    stages = []
-    for axis in ("dp", "ctx"):
-        bits = mesh_shape[axis].bit_length() - 1
-        shift = 0
-        while bits > 0:
-            take = min(2, bits)
-            stages.append((axis, shift, 1 << take))
-            shift += take
-            bits -= take
-    return stages
+    dp, ctx = mesh_shape["dp"], mesh_shape["ctx"]
+    near = min(4, dp)
+    stages = [(0, near, 0, 2), (2, dp // near, 0, 1)]
+    rest, bit = ctx // 2, 1
+    while rest > 1:
+        size = min(4, rest)
+        stages.append((0, 1, bit, size))
+        rest, bit = rest // size, bit + 2
+    return [stage for stage in stages if stage[1] * stage[3] > 1]
 
 
 def nt(a, b):
@@ -62,7 +94,7 @@
     q_ref, k_ref, v_ref, cot_ref, aux_ref, cen_ref,
     dq_ref, dk_ref, dv_ref, core_ref,
     kv, qbuf, dabuf, dasend, atx, atin, dqx, csend, crecv, finx, arbuf,
-    cots, est, mat, cent, kt, vt, dat, sc, ph, ds, part,
+    cots, est, mat, cent, cenw, kt, vt, dat, sc, ph, ds, part,
     kx_s, kx_r, loc, qx_s, qx_r, qloc, hop_s, hop_r, da_s, da_r, at_s, at_r,
     dq_s, dq_r, ch_s, ch_r, fin_s, fin_r, ar_s, ar_r,
 ):
@@ -74,16 +106,21 @@
     partner = {"ctx": me + 1 - 2 * xlo}
     up = {"ctx": lax.rem(me + 2, n_ctx)}
     down = {"ctx": lax.rem(me + n_ctx - 2, n_ctx)}
-    at_axis = {"dp": me_dp, "ctx": me}
 
     def stage_peers(stage):
-        axis, shift, size = stage
-        here = at_axis[axis]
-        pos = lax.rem(here // (1 << shift), size)
+        dp_bit, dp_size, ctx_bit, ctx_size = stage
+        size = dp_size * ctx_size
+        dp_pos = lax.rem(me_dp // (1 << dp_bit), dp_size)
+        ctx_pos = lax.rem(me // (1 << ctx_bit), ctx_size)
+        pos = dp_pos * ctx_size + ctx_pos
         out = []
         for d in range(1, size):
             their = lax.rem(pos + d, size)
-            out.append((d, {axis: here + (their - pos) * (1 << shift)}))
+            dev = {
+                "dp": me_dp + (their // ctx_size - dp_pos) * (1 << dp_bit),
+                "ctx": me + (lax.rem(their, ctx_size) - ctx_pos) * (1 << ctx_bit),
+            }
+            out.append((d, dev))
         return pos, out
 
     def remote(src, dst, s, r, dev):
@@ -123,8 +160,8 @@
             q_ref.at[:, lanes(xlo * 2 * OWN + 2 * h + g)], qbuf.at[h, rows(2 * g + xlo)], qloc.at[h, g]
         )
 
-    def hop(s, h):
-        return remote(kv.at[s - 1, h], kv.at[s, h], hop_s.at[s - 1, h], hop_r.at[s - 1, h], up)
+    def hop(s, h, c):
+        return remote(kv.at[s - 1, h, c], kv.at[s, h, c], hop_s.at[s - 1, h, c], hop_r.at[s - 1, h, c], up)
 
     def dax(h, g):
         return remote(
@@ -142,8 +179,10 @@
             dq_s.at[h, g], dq_r.at[h, g], partner,
         )
 
-    def chain(st, h):
-        return remote(csend.at[st, h], crecv.at[st, h], ch_s.at[st, h], ch_r.at[st, h], down)
+    def chain(st, h, c):
+        return remote(
+            csend.at[st, h, c], crecv.at[st, h, c], ch_s.at[st, h, c], ch_r.at[st, h, c], down
+        )
 
     outs = (dk_ref, dv_ref)
 
@@ -161,10 +200,9 @@
             qx(h, c).start()
             qlocal(h, c).start()
 
-    for t_pad in range(1):
-        @pl.loop(0, TOK)
-        def _(t):
-            cots[pl.ds(t * JP + JP - 8, 8), :] = jnp.zeros((8, HD), F32)
+    @pl.loop(0, TOK)
+    def _(t):
+        cots[pl.ds(t * JP + JP - 8, 8), :] = jnp.zeros((8, HD), F32)
 
     @pl.loop(0, J1)
     def _(j):
@@ -173,90 +211,97 @@
     @pl.loop(0, BOND)
     def _(b):
         cent[rows(b), :] = cen_ref[b].T
+        cenw[:, lanes(b)] = cen_ref[b]
 
     def cot_tok(t):
         return cots[pl.ds(pl.multiple_of(t * JP, JP), JP), :].astype(BF16)
 
     def e_terms(t):
-        e = nn(aux_ref[...], cot_tok(t)).astype(BF16)
-        r16 = pl.ds(pl.multiple_of(t * HQ, HQ), HQ)
-        for b in range(BOND):
-            est[r16, b * HD : (b + 1) * HD] = e[b * HQ : (b + 1) * HQ]
-
-    order = sorted(((s, h) for s in range(1, HOPS + 1) for h in range(OWN)), key=lambda a: (a[0] + a[1], -a[0]))
-    per = TOK // len(order)
-    for n, (s, h) in enumerate(order):
+        e = nn(aux_ref[...], jnp.concatenate([cot_tok(t), cot_tok(t + 1)], axis=1)).astype(BF16)
+        for u in range(2):
+            r16 = pl.ds(pl.multiple_of((t + u) * HQ, HQ), HQ)
+            for b in range(BOND):
+                est[r16, b * HD : (b + 1) * HD] = e[b * HQ : (b + 1) * HQ, u * HD : (u + 1) * HD]
+
+    def forward(s, h, c):
         if s == 1:
-            for c in range(2):
-                kx(h, c).wait_recv()
-                kloc(h, c).wait()
+            kx(h, c).wait_recv()
+            kloc(h, c).wait()
         else:
-            hop(s - 1, h).wait_recv()
-        hop(s, h).start()
-
-        @pl.loop(n * per, (n + 1) * per, unroll=4)
-        def _(t):
-            e_terms(t)
-
-    @pl.loop(0, 8)
-    def _(n):
-        rr = pl.ds(pl.multiple_of(n * 256, 256), 256)
-        mat[rr, :] = nn(est[rr, :], cent[...]).astype(BF16).astype(F32)
-
-    for h in range(OWN):
-        for g in range(2):
-            i_other = other * 2 * OWN + 2 * h + g
-            dasend[h, g] = mat[pl.ds(i_other, TOK, stride=HQ), :].astype(BF16)
-    for h in range(OWN):
-        for g in range(2):
-            dax(h, g).start()
-    for h in range(OWN):
-        for g in range(2):
-            i_own = xlo * 2 * OWN + 2 * h + g
-            dabuf[h, rows(2 * g + xlo)] = mat[pl.ds(i_own, TOK, stride=HQ), :].astype(BF16)
-
-    for h in range(OWN):
+            hop(s - 1, h, c).wait_recv()
+        hop(s, h, c).start()
+
+    def d_terms():
+        @pl.loop(0, 8)
+        def _(n):
+            rr = pl.ds(pl.multiple_of(n * 256, 256), 256)
+            mat[rr, :] = nn(est[rr, :], cent[...]).astype(BF16).astype(F32)
+
+        for h in range(OWN):
+            for g in range(2):
+                i_other = other * 2 * OWN + 2 * h + g
+                dasend[h, g] = mat[pl.ds(i_other, TOK, stride=HQ), :].astype(BF16)
+        for h in range(OWN):
+            for g in range(2):
+                dax(h, g).start()
+        for h in range(OWN):
+            for g in range(2):
+                i_own = xlo * 2 * OWN + 2 * h + g
+                dabuf[h, rows(2 * g + xlo)] = mat[pl.ds(i_own, TOK, stride=HQ), :].astype(BF16)
+
+    pieces = TOK // FIRST.count("e")
+    done = 0
+    for item in FIRST:
+        if item == "e":
+
+            @pl.loop(done // 2, (done + pieces) // 2, unroll=4)
+            def _(n):
+                e_terms(2 * n)
+
+            done += pieces
+        elif item == "d":
+            d_terms()
+        else:
+            forward(*item[1:])
+
+    t_pos = lax.rem(lax.broadcasted_iota(jnp.int32, (TOK, COLS), 1), BLK)
+    r_iota = lax.broadcasted_iota(jnp.int32, (TOK, COLS), 0)
+
+    def back(st, hh, c):
+        total = part[hh, HOPS - st, c]
+        if st > 0:
+            chain(st - 1, hh, c).wait_recv()
+            total = crecv[st - 1, hh, c].astype(F32) + total
+        total = total.astype(BF16)
+        if st < HOPS:
+            csend[st, hh, c] = total
+            chain(st, hh, c).start()
+        else:
+            part[hh, 0, c] = total.astype(F32)
+            finx[hh, c] = part[hh, 0, c, rows(other)].astype(BF16)
+            finc(hh, c).start()
+            outs[c][:, lanes(xlo * OWN + hh)] = part[hh, 0, c, rows(xlo)].astype(BF16)
+
+    def hook(h, name):
+        for (n, point), todo in HOOKS.items():
+            if point == name:
+
+                @pl.when(h == n)
+                def _():
+                    for item in todo:
+                        if item[0] == "f":
+                            forward(*item[1:])
+                        else:
+                            back(*item[1:])
+
+    @pl.loop(0, OWN)
+    def _(h):
         for g in range(2):
             qx(h, g).wait_recv()
             qlocal(h, g).wait()
-            dax(h, g).wait_recv()
-
-    t_pos = lax.rem(lax.broadcasted_iota(jnp.int32, (TOK, COLS), 1), BLK)
-    r_iota = lax.broadcasted_iota(jnp.int32, (TOK, COLS), 0)
-
-    def service(n):
-        for st in range(HOPS + 1):
-            hh = n - st
-
-            @pl.when(jnp.logical_and(hh >= 0, hh < OWN))
-            def _():
-                if st == 0:
-                    total = part[hh, HOPS]
-                else:
-                    chain(st - 1, hh).wait_recv()
-                    total = crecv[st - 1, hh].astype(F32) + part[hh, HOPS - st]
-                total = total.astype(BF16)
-                if st < HOPS:
-                    csend[st, hh] = total
-                    chain(st, hh).start()
-                else:
-                    part[hh, 0] = total.astype(F32)
-                    for c in range(2):
-                        finx[hh, c] = part[hh, 0, c, rows(other)].astype(BF16)
-                        finc(hh, c).start()
-                        outs[c][:, lanes(xlo * OWN + hh)] = part[hh, 0, c, rows(xlo)].astype(BF16)
-
-    @pl.loop(0, OWN)
-    def _(h):
-        hop(HOPS, h).wait_recv()
+        hop(HOPS, h, 0).wait_recv()
         qh = qbuf[h]
-        dah = dabuf[h]
-        dat[...] = dah.T
-        for s in range(HOPS + 1):
-            for u in range(2):
-                w = 2 * s + u
-                kt[:, w * TOK : (w + 1) * TOK] = kv[s, h, 0, u * TOK : (u + 1) * TOK].T
-                vt[:, w * TOK : (w + 1) * TOK] = kv[s, h, 1, u * TOK : (u + 1) * TOK].T
+        hook(h, "a")
 
         def scores(s, u):
             return nt(kv[s, h, 0, rows(u)], qh)
@@ -277,6 +322,8 @@
 
         m = lax.fori_loop(2, 2 * HOPS, score_step, m)
 
+        hook(h, "b")
+
         def exp_step(w, l):
             e = jnp.exp2((sc[rows(w), :] - m) * EXP_SCALE)
             sc[rows(w), :] = e
@@ -284,6 +331,12 @@
 
         l = lax.fori_loop(0, 2 * HOPS, exp_step, jnp.zeros((1, COLS), F32))
         inv = 1.0 / l
+        hook(h, "c")
+        hop(HOPS, h, 1).wait_recv()
+        for s in range(HOPS + 1):
+            for u in range(2):
+                w = 2 * s + u
+                vt[:, w * TOK : (w + 1) * TOK] = kv[s, h, 1, u * TOK : (u + 1) * TOK].T
 
         for u in range(2):
             causal = t_pos >= r_iota + u * TOK
@@ -299,11 +352,24 @@
             sc[rows(w), :] = p
             ph[rows(w), :] = p.astype(BF16)
 
+        hook(h, "d")
+        for g in range(2):
+            dax(h, g).wait_recv()
+        dah = dabuf[h]
+        dat[...] = dah.T
         att = nn(vt[...], ph[...]).astype(BF16)
         delta = jnp.sum(att.astype(F32) * dat[...].astype(F32), axis=0, keepdims=True)
         atx[h] = att.T
         for g in range(2):
             attnx(h, g).start()
+        hook(h, "e")
+
+        @pl.loop(0, HOPS + 1)
+        def _(s):
+            for u in range(2):
+                part[h, s, 1, u * TOK : (u + 1) * TOK] = nn(ph[rows(2 * s + u), :], dah)
+
+        hook(h, "f")
 
         def dprob(s, u):
             return nn(kv[s, h, 1, rows(u)], dat[...])
@@ -321,6 +387,11 @@
             dp = dprob(w // 2, lax.rem(w, 2))
             ds[rows(w), :] = (sc[rows(w), :] * (dp - delta)).astype(BF16)
 
+        hook(h, "g")
+        for s in range(HOPS + 1):
+            for u in range(2):
+                w = 2 * s + u
+                kt[:, w * TOK : (w + 1) * TOK] = kv[s, h, 0, u * TOK : (u + 1) * TOK].T
         dqt = (nn(kt[...], ds[...]) * SCORE_SCALE).astype(BF16)
         dqx[h] = dqt.T
         for g in range(2):
@@ -331,61 +402,78 @@
         @pl.loop(0, HOPS + 1)
         def _(s):
             for u in range(2):
-                rr = rows(2 * s + u)
-                part[h, s, 0, u * TOK : (u + 1) * TOK] = nn(ds[rr, :], qh) * SCORE_SCALE
-                part[h, s, 1, u * TOK : (u + 1) * TOK] = nn(ph[rr, :], dah)
-
-        service(h)
-
-    service(OWN)
-
-    for h in range(OWN):
-        for g in range(2):
-            i_own = xlo * 2 * OWN + 2 * h + g
-            mat[pl.ds(i_own, TOK, stride=HQ), :] = atx[h, rows(2 * g + xlo)].astype(F32)
-    for h in range(OWN):
-        for g in range(2):
-            attnx(h, g).wait_recv()
-            i_other = other * 2 * OWN + 2 * h + g
-            mat[pl.ds(i_other, TOK, stride=HQ), :] = atin[h, g].astype(F32)
-
-    @pl.loop(0, 8)
-    def _(n):
-        rr = pl.ds(pl.multiple_of(n * 256, 256), 256)
-        a = mat[rr, :].astype(BF16)
-        for b in range(BOND):
-            est[rr, b * HD : (b + 1) * HD] = nn(a, cen_ref[b]).astype(BF16)
-
-    service(OWN + 1)
-
-    def core_step(t, acc):
-        r16 = pl.ds(pl.multiple_of(t * HQ, HQ), HQ)
-        f = jnp.concatenate([est[r16, b * HD : (b + 1) * HD] for b in range(BOND)], axis=0)
-        return acc + nt(cot_tok(t), f)
-
-    core_ref[...] = lax.fori_loop(0, TOK, core_step, jnp.zeros((JP, BOND * HQ), F32), unroll=4)
-
-    for k, stage in enumerate(stages):
-        pos, peers = stage_peers(stage)
+                part[h, s, 0, u * TOK : (u + 1) * TOK] = nn(ds[rows(2 * s + u), :], qh) * SCORE_SCALE
+
+        hook(h, "h")
+
+    def attn_terms():
+        for h in range(OWN):
+            for g in range(2):
+                i_own = xlo * 2 * OWN + 2 * h + g
+                mat[pl.ds(i_own, TOK, stride=HQ), :] = atx[h, rows(2 * g + xlo)].astype(F32)
+        for h in range(OWN):
+            for g in range(2):
+                attnx(h, g).wait_recv()
+                i_other = other * 2 * OWN + 2 * h + g
+                mat[pl.ds(i_other, TOK, stride=HQ), :] = atin[h, g].astype(F32)
+
+    def f_terms(lo, hi):
+        @pl.loop(lo, hi)
+        def _(n):
+            rr = pl.ds(pl.multiple_of(n * 256, 256), 256)
+            est[rr, :] = nn(mat[rr, :].astype(BF16), cenw[...]).astype(BF16)
+
+    def core_step(n, acc):
+        def f_tok(t):
+            r16 = pl.ds(pl.multiple_of(t * HQ, HQ), HQ)
+            return jnp.concatenate([est[r16, b * HD : (b + 1) * HD] for b in range(BOND)], axis=0)
+
+        cot2 = jnp.concatenate([cot_tok(2 * n), cot_tok(2 * n + 1)], axis=1)
+        return acc + nt(cot2, jnp.concatenate([f_tok(2 * n), f_tok(2 * n + 1)], axis=1))
+
+    def reduce_copy(k, d, dev):
+        pos = stage_peers(stages[k])[0]
+        return remote(arbuf.at[k, pos], arbuf.at[k, pos], ar_s.at[k, d], ar_r.at[k, d], dev)
+
+    def reduce_start(k):
+        pos, peers = stage_peers(stages[k])
         arbuf[k, pos] = core_ref[...]
-
-        def copy(d, dev):
-            return remote(arbuf.at[k, pos], arbuf.at[k, pos], ar_s.at[k, d], ar_r.at[k, d], dev)
-
         for d, dev in peers:
-            copy(d, dev).start()
-        if k < OWN - 2:
-            service(OWN + 2 + k)
-        for d, dev in peers:
-            copy(d, dev).wait_recv()
+            reduce_copy(k, d, dev).start()
+
+    def reduce_end(k):
+        for d, dev in stage_peers(stages[k])[1]:
+            reduce_copy(k, d, dev).wait_recv()
         total = arbuf[k, 0]
-        for n in range(1, stage[2]):
+        for n in range(1, stages[k][1] * stages[k][3]):
             total = total + arbuf[k, n]
         core_ref[...] = total
-        for d, dev in peers:
-            copy(d, dev).wait_send()
-    for k in range(max(0, min(OWN - 2, len(stages))), OWN - 2):
-        service(OWN + 2 + k)
+        for d, dev in stage_peers(stages[k])[1]:
+            reduce_copy(k, d, dev).wait_send()
+
+    core_ref[...] = jnp.zeros((JP, BOND * HQ), F32)
+    n_f = LAST.count("f")
+    n_g = LAST.count("g")
+    f_done = g_done = 0
+    reduced = -1
+    for item in LAST:
+        if item == "f":
+            if f_done == 0:
+                attn_terms()
+            f_terms(f_done * 8 // n_f, (f_done + 1) * 8 // n_f)
+            f_done += 1
+        elif item == "g":
+            lo, hi = g_done * TOK // 2 // n_g, (g_done + 1) * TOK // 2 // n_g
+            core_ref[...] = lax.fori_loop(lo, hi, core_step, core_ref[...], unroll=4)
+            g_done += 1
+        elif item[0] == "b":
+            back(*item[1:])
+        elif item[1] < len(stages):
+            if reduced >= 0:
+                reduce_end(reduced)
+            reduced = item[1]
+            reduce_start(reduced)
+    reduce_end(reduced)
 
     for h in range(OWN):
         for c in range(2):
@@ -395,9 +483,9 @@
             attnx(h, c).wait_send()
             dqxc(h, c).wait()
             finc(h, c).wait()
-        for s in range(HOPS):
-            hop(s + 1, h).wait_send()
-            chain(s, h).wait_send()
+            for s in range(HOPS):
+                hop(s + 1, h, c).wait_send()
+                chain(s, h, c).wait_send()
 
 
 def solution(mesh):
@@ -412,7 +500,7 @@
         dma = pltpu.SemaphoreType.DMA
         pair = dma((OWN, 2))
         width = 2 * OWN * HD
-        most = max(size for _, _, size in stages)
+        most = max(stage[1] * stage[3] for stage in stages)
         dq, dk, dv, core = pl.pallas_call(
             functools.partial(kernel, n_ctx, stages),
             out_shape=(
@@ -439,6 +527,7 @@
                 pltpu.VMEM((TOK * HQ, BOND * HD), BF16),
                 pltpu.VMEM((TOK * HQ, HD), F32),
                 pltpu.VMEM((BOND * HD, HD), BF16),
+                pltpu.VMEM((HD, BOND * HD), BF16),
                 pltpu.VMEM((HD, (HOPS + 1) * BLK), BF16),
                 pltpu.VMEM((HD, (HOPS + 1) * BLK), BF16),
                 pltpu.VMEM((HD, COLS), BF16),
@@ -447,9 +536,9 @@
                 pltpu.VMEM(((HOPS + 1) * BLK, COLS), BF16),
                 pltpu.VMEM((OWN, HOPS + 1, 2, BLK, HD), F32),
                 pair, pair, pair, pair, pair, pair,
-                dma((HOPS, OWN)), dma((HOPS, OWN)),
+                dma((HOPS, OWN, 2)), dma((HOPS, OWN, 2)),
                 pair, pair, pair, pair, pair, pair,
-                dma((HOPS, OWN)), dma((HOPS, OWN)),
+                dma((HOPS, OWN, 2)), dma((HOPS, OWN, 2)),
                 pair, pair,
                 dma((len(stages), most)), dma((len(stages), most)),
             ],

time: 164 us -> 118 us (0.72)
  Pallas kernels: 156 us -> 109 us
    pallas_call x1, Pallas kernels: 156 us -> 109 us  [step(): pl.pallas_call(functools.partial(kernel, n_ctx, stages), out_shape=(jax.S...]
where the time goes in v2:
time: 118 us; the launch traced here: 116 us
  Pallas kernels  109 us (92%)
  local copies, waits for them, and re-layouts  5.44 us (5%)
    pallas_call x1, Pallas kernels, step(): pl.pallas_call(functools.partial(kernel, n_ctx, stages), out_shape=(jax.S...  109 us
    unnamed x8, local copies, waits for them, and re-layouts  3.95 us

profile of v2, /device:TPU:6, one launch (start us, length us, event | category | flops | bytes accessed | tf_op | source)
XLA Modules:
  0.0 116.3 jit_solution(11111985568096603502)
XLA Ops:
  0.6 0.8 copy.12
  1.4 0.6 pad.4.aux_ref
  2.0 109.4 %shard_map.93 = (bf16[128,2048]{1,0:T(8,128)(2,1)}, bf16[128,1024]{1,0:T(8,128)(2,1)}, bf16[128,1024]{1,0:T(8,128)(2,1)}, f32[48,128]{1,0:T(8,128)}) custom-call(bf16[128,2048]{1,0:T(8,128)(2,1)} %bitcast.14, bf16[128,1024]{1,0:T(8,128)(2,1)} %bitcast.18, bf16[128,1024]{1,0:T(8,128)(2,1)} %bitcast.19, bf16[128,5376]{1,0:T(8,128)(2,1)} %bitcast.12, ...), custom_call_target="tpu_custom_call" | custom-call | tf_op jit(solution)/shard_map/pallas_call | solution.py:504
  111.4 0.0 copy-start.1
  111.4 0.0 copy-start
  111.4 0.8 slice_multiply_fusion
  112.2 0.1 copy.13
  112.3 0.7 copy.14
  113.0 1.9 %copy.18 = bf16[1,128,2048]{2,1,0:T(8,128)(2,1)} copy(bf16[1,128,2048]{2,1,0:T(8,128)(2,1)} %bitcast.13) | data formatting | bytes 1048576
  114.9 0.0 copy-done.1
  114.9 0.7 copy.19
  115.6 0.0 copy-done
  115.6 0.7 copy.20
Async XLA Ops:
  111.4 3.5 %copy-start.1 = (bf16[128,1024]{1,0:T(8,128)(2,1)S(1)}, bf16[128,1024]{1,0:T(8,128)(2,1)}, u32[]{:S(2)}) copy-start(bf16[128,1024]{1,0:T(8,128)(2,1)} %get-tuple-element.9) | copy-start | bytes 786436
  111.4 4.2 %copy-start = (bf16[128,1024]{1,0:T(8,128)(2,1)S(1)}, bf16[128,1024]{1,0:T(8,128)(2,1)}, u32[]{:S(2)}) copy-start(bf16[128,1024]{1,0:T(8,128)(2,1)} %get-tuple-element.10) | copy-start | bytes 786436

commit v3 on v2

--- a/solution.py
+++ b/solution.py
@@ -26,38 +26,44 @@
 F32 = jnp.float32
 BF16 = jnp.bfloat16
 MESH = pl.DeviceIdType.MESH
+SPLIT = 2
+PIECES_A = 2
+PIECES_G = 4
 
 FIRST = [
-    "e", "e", "e", "e", ("f", 1, 0, 0), "e", "e", "e", ("f", 1, 0, 1), "e", "e", "e", ("f", 1, 1, 0), "e",
-    "e", "e", "e", ("f", 2, 0, 0), "e", "e", "d", ("f", 2, 0, 1), ("f", 1, 1, 1), ("f", 3, 0, 0),
-    ("f", 3, 0, 1), ("f", 2, 1, 0), ("f", 4, 0, 0), ("f", 4, 0, 1), ("f", 2, 1, 1), ("f", 3, 1, 0),
+    "e", "e", "e", "e", ("f", 1, 0, 0), ("f", 1, 0, 1), ("f", 1, 1, 0), ("f", 1, 1, 1), ("f", 1, 2, 0),
+    ("f", 2, 0, 0), "e", "e", ("f", 2, 0, 1), "e", ("f", 2, 1, 0), "e", "e", ("f", 3, 0, 0), "e",
+    ("f", 3, 0, 1), "e", "e", ("f", 2, 1, 1), "e", "e", "e", ("f", 4, 0, 0), "e", ("f", 4, 0, 1),
+    ("f", 3, 1, 0), "d", ("f", 3, 1, 1), ("f", 1, 2, 1),
 ]
 HOOKS = {
-    (0, "b"): [("f", 1, 2, 0)],
-    (0, "e"): [("f", 3, 1, 1)],
+    (0, "e"): [("f", 4, 1, 0)],
     (0, "f"): [("b", 0, 0, 1)],
-    (0, "g"): [("f", 4, 1, 0)],
-    (0, "h"): [("f", 1, 2, 1), ("b", 0, 0, 0), ("f", 4, 1, 1), ("b", 1, 0, 1), ("f", 2, 2, 0)],
-    (1, "b"): [("b", 1, 0, 0), ("f", 2, 2, 1)],
-    (1, "c"): [("f", 1, 3, 0)],
-    (1, "d"): [("b", 2, 0, 1)],
-    (1, "f"): [("f", 3, 2, 0)],
-    (1, "g"): [("b", 0, 1, 1), ("f", 3, 2, 1)],
-    (1, "h"): [("b", 0, 1, 0), ("f", 1, 3, 1), ("b", 2, 0, 0), ("f", 4, 2, 0), ("b", 1, 1, 1), ("f", 4, 2, 1), ("b", 1, 1, 0), ("f", 2, 3, 0), ("b", 3, 0, 1), ("f", 2, 3, 1)],
-    (2, "b"): [("b", 2, 1, 1)],
-    (2, "d"): [("b", 2, 1, 0)],
-    (2, "e"): [("f", 3, 3, 0)],
-    (2, "g"): [("f", 3, 3, 1), ("b", 0, 2, 1), ("b", 3, 0, 0), ("b", 4, 0, 1)],
-    (2, "h"): [("f", 4, 3, 0), ("b", 0, 2, 0), ("f", 4, 3, 1), ("b", 1, 2, 1), ("b", 3, 1, 1), ("b", 3, 1, 0), ("b", 4, 0, 0)],
-    (3, "c"): [("b", 1, 2, 0)],
-    (3, "f"): [("b", 0, 3, 1), ("b", 2, 2, 1), ("b", 4, 1, 1)],
-    (3, "g"): [("b", 4, 1, 0)],
+    (0, "g"): [("f", 4, 1, 1)],
+    (0, "h"): [("b", 0, 0, 0), ("f", 2, 2, 0), ("f", 2, 2, 1), ("f", 1, 3, 0)],
+    (1, "b"): [("b", 1, 0, 1)],
+    (1, "c"): [("f", 1, 3, 1)],
+    (1, "d"): [("b", 1, 0, 0)],
+    (1, "e"): [("f", 3, 2, 0)],
+    (1, "f"): [("b", 0, 1, 1)],
+    (1, "g"): [("b", 2, 0, 1), ("f", 3, 2, 1), ("f", 2, 3, 0)],
+    (1, "h"): [("b", 0, 1, 0), ("b", 1, 1, 1), ("f", 4, 2, 0), ("f", 2, 3, 1), ("A", 0, 0), ("b", 2, 0, 0), ("A", 0, 1), ("f", 4, 2, 1), ("G", 0, 0), ("b", 1, 1, 0), ("b", 3, 0, 1), ("G", 0, 1), ("f", 3, 3, 0)],
+    (2, "a"): [("b", 2, 1, 1)],
+    (2, "b"): [("b", 3, 0, 0), ("f", 3, 3, 1)],
+    (2, "e"): [("b", 2, 1, 0), ("f", 4, 3, 0)],
+    (2, "f"): [("b", 0, 2, 1)],
+    (2, "g"): [("b", 3, 1, 1), ("f", 4, 3, 1)],
+    (2, "h"): [("b", 0, 2, 0)],
+    (3, "b"): [("b", 3, 1, 0), ("b", 1, 2, 1)],
+    (3, "f"): [("b", 0, 3, 1)],
+    (3, "g"): [("b", 1, 2, 0)],
 }
 LAST = [
-    "f", ("b", 0, 3, 0), "f", "f", ("b", 1, 3, 1), "f", "g", ("b", 2, 2, 0), "g", "g", ("b", 1, 3, 0), "g",
-    "g", ("b", 2, 3, 1), "g", "g", ("b", 3, 2, 1), "g", ("a", 0), ("b", 2, 3, 0), ("b", 3, 2, 0), ("a", 1),
-    ("b", 3, 3, 1), ("b", 4, 2, 1), ("b", 3, 3, 0), ("b", 4, 2, 0), ("a", 2), ("b", 4, 3, 1), ("b", 4, 3, 0),
-    ("a", 3),
+    ("b", 0, 3, 0), ("b", 2, 2, 1), ("G", 0, 2), ("G", 0, 3), ("b", 1, 3, 1), ("A", 1, 0), ("b", 4, 0, 0),
+    ("A", 1, 1), ("b", 2, 2, 0), ("G", 1, 0), ("G", 1, 1), ("b", 1, 3, 0), ("G", 1, 2), ("b", 3, 2, 1),
+    ("G", 1, 3), ("b", 2, 3, 1), ("a", 0), ("b", 2, 3, 0), ("a", 1), ("b", 3, 2, 0), ("b", 4, 2, 1),
+    ("b", 4, 0, 1), ("b", 4, 1, 0), ("b", 3, 3, 1), ("a", 2), ("b", 3, 3, 0), ("b", 4, 2, 0), ("b", 4, 1, 1),
+    ("b", 4, 3, 1), ("b", 4, 3, 0), ("a", 3),
 ]
 
 
@@ -94,9 +100,9 @@
     q_ref, k_ref, v_ref, cot_ref, aux_ref, cen_ref,
     dq_ref, dk_ref, dv_ref, core_ref,
     kv, qbuf, dabuf, dasend, atx, atin, dqx, csend, crecv, finx, arbuf,
-    cots, est, mat, cent, cenw, kt, vt, dat, sc, ph, ds, part,
+    aux, cots, est, fst, gacc, mat, cent, cenw, kt, vt, dat, sc, ph, ds, part,
     kx_s, kx_r, loc, qx_s, qx_r, qloc, hop_s, hop_r, da_s, da_r, at_s, at_r,
-    dq_s, dq_r, ch_s, ch_r, fin_s, fin_r, ar_s, ar_r,
+    dq_s, dq_r, ch_s, ch_r, fin_s, fin_r, ar_s, ar_r, own_s, own_r,
 ):
     me_dp = lax.axis_index("dp")
     me = lax.axis_index("ctx")
@@ -130,7 +136,7 @@
 
     barrier = pltpu.get_barrier_semaphore()
     greet = [partner, up, down]
-    for stage in stages:
+    for stage in (stage for stage in stages if stage[2] == 0):
         greet += [dev for _, dev in stage_peers(stage)[1]]
     for dev in greet:
         pl.semaphore_signal(barrier, inc=1, device_id=dev, device_id_type=MESH)
@@ -160,6 +166,18 @@
             q_ref.at[:, lanes(xlo * 2 * OWN + 2 * h + g)], qbuf.at[h, rows(2 * g + xlo)], qloc.at[h, g]
         )
 
+    def own(h, c):
+        return remote(
+            srcs[c].at[:, lanes(xlo * OWN + h)], kv.at[1, h, c, rows(xlo)],
+            own_s.at[h, c], own_r.at[h, c], up,
+        )
+
+    def rest(h, c):
+        return remote(
+            kv.at[0, h, c, rows(other)], kv.at[1, h, c, rows(other)],
+            hop_s.at[0, h, c], hop_r.at[0, h, c], up,
+        )
+
     def hop(s, h, c):
         return remote(kv.at[s - 1, h, c], kv.at[s, h, c], hop_s.at[s - 1, h, c], hop_r.at[s - 1, h, c], up)
 
@@ -195,11 +213,17 @@
         for c in range(2):
             kx(h, c).start()
             kloc(h, c).start()
+            if h < SPLIT:
+                own(h, c).start()
     for h in range(OWN):
         for c in range(2):
             qx(h, c).start()
             qlocal(h, c).start()
 
+    aux[...] = jnp.zeros(aux.shape, BF16)
+    aux[:, :J1] = aux_ref[...]
+    gacc[...] = jnp.zeros(gacc.shape, F32)
+
     @pl.loop(0, TOK)
     def _(t):
         cots[pl.ds(t * JP + JP - 8, 8), :] = jnp.zeros((8, HD), F32)
@@ -217,7 +241,7 @@
         return cots[pl.ds(pl.multiple_of(t * JP, JP), JP), :].astype(BF16)
 
     def e_terms(t):
-        e = nn(aux_ref[...], jnp.concatenate([cot_tok(t), cot_tok(t + 1)], axis=1)).astype(BF16)
+        e = nn(aux[...], jnp.concatenate([cot_tok(t), cot_tok(t + 1)], axis=1)).astype(BF16)
         for u in range(2):
             r16 = pl.ds(pl.multiple_of((t + u) * HQ, HQ), HQ)
             for b in range(BOND):
@@ -227,9 +251,15 @@
         if s == 1:
             kx(h, c).wait_recv()
             kloc(h, c).wait()
+        elif s == 2 and h < SPLIT:
+            own(h, c).wait_recv()
+            rest(h, c).wait_recv()
         else:
             hop(s - 1, h, c).wait_recv()
-        hop(s, h, c).start()
+        if s == 1 and h < SPLIT:
+            rest(h, c).start()
+        else:
+            hop(s, h, c).start()
 
     def d_terms():
         @pl.loop(0, 8)
@@ -282,6 +312,38 @@
             finc(hh, c).start()
             outs[c][:, lanes(xlo * OWN + hh)] = part[hh, 0, c, rows(xlo)].astype(BF16)
 
+    def attn_terms(grp):
+        for h in (2 * grp, 2 * grp + 1):
+            for g in range(2):
+                q = h % 2 * 2 + g
+                mat[pl.ds(xlo * OWN + q, TOK, stride=HQ // 2), :] = atx[h, rows(2 * g + xlo)].astype(F32)
+                attnx(h, g).wait_recv()
+                mat[pl.ds(other * OWN + q, TOK, stride=HQ // 2), :] = atin[h, g].astype(F32)
+
+    def f_terms(n):
+        @pl.loop(n * 4 // PIECES_A, (n + 1) * 4 // PIECES_A)
+        def _(m):
+            rr = pl.ds(pl.multiple_of(m * 256, 256), 256)
+            fst[rr, :] = nn(mat[rr, :].astype(BF16), cenw[...]).astype(BF16).astype(F32)
+
+    def core_step(n, acc):
+        def f_tok(t):
+            r8 = pl.ds(pl.multiple_of(t * 8, 8), 8)
+            return jnp.concatenate([fst[r8, b * HD : (b + 1) * HD] for b in range(BOND)], axis=0)
+
+        cot4 = jnp.concatenate([cot_tok(4 * n + u) for u in range(4)], axis=1)
+        return acc + nt(cot4, jnp.concatenate([f_tok(4 * n + u).astype(BF16) for u in range(4)], axis=1))
+
+    def core_piece(item):
+        kind, grp, n = item
+        if kind == "A":
+            if n == 0:
+                attn_terms(grp)
+            f_terms(n)
+        else:
+            steps = TOK // 4 // PIECES_G
+            gacc[grp] = lax.fori_loop(n * steps, (n + 1) * steps, core_step, gacc[grp], unroll=2)
+
     def hook(h, name):
         for (n, point), todo in HOOKS.items():
             if point == name:
@@ -291,6 +353,8 @@
                     for item in todo:
                         if item[0] == "f":
                             forward(*item[1:])
+                        elif item[0] in "AG":
+                            core_piece(item)
                         else:
                             back(*item[1:])
 
@@ -406,31 +470,6 @@
 
         hook(h, "h")
 
-    def attn_terms():
-        for h in range(OWN):
-            for g in range(2):
-                i_own = xlo * 2 * OWN + 2 * h + g
-                mat[pl.ds(i_own, TOK, stride=HQ), :] = atx[h, rows(2 * g + xlo)].astype(F32)
-        for h in range(OWN):
-            for g in range(2):
-                attnx(h, g).wait_recv()
-                i_other = other * 2 * OWN + 2 * h + g
-                mat[pl.ds(i_other, TOK, stride=HQ), :] = atin[h, g].astype(F32)
-
-    def f_terms(lo, hi):
-        @pl.loop(lo, hi)
-        def _(n):
-            rr = pl.ds(pl.multiple_of(n * 256, 256), 256)
-            est[rr, :] = nn(mat[rr, :].astype(BF16), cenw[...]).astype(BF16)
-
-    def core_step(n, acc):
-        def f_tok(t):
-            r16 = pl.ds(pl.multiple_of(t * HQ, HQ), HQ)
-            return jnp.concatenate([est[r16, b * HD : (b + 1) * HD] for b in range(BOND)], axis=0)
-
-        cot2 = jnp.concatenate([cot_tok(2 * n), cot_tok(2 * n + 1)], axis=1)
-        return acc + nt(cot2, jnp.concatenate([f_tok(2 * n), f_tok(2 * n + 1)], axis=1))
-
     def reduce_copy(k, d, dev):
         pos = stage_peers(stages[k])[0]
         return remote(arbuf.at[k, pos], arbuf.at[k, pos], ar_s.at[k, d], ar_r.at[k, d], dev)
@@ -451,26 +490,17 @@
         for d, dev in stage_peers(stages[k])[1]:
             reduce_copy(k, d, dev).wait_send()
 
-    core_ref[...] = jnp.zeros((JP, BOND * HQ), F32)
-    n_f = LAST.count("f")
-    n_g = LAST.count("g")
-    f_done = g_done = 0
     reduced = -1
     for item in LAST:
-        if item == "f":
-            if f_done == 0:
-                attn_terms()
-            f_terms(f_done * 8 // n_f, (f_done + 1) * 8 // n_f)
-            f_done += 1
-        elif item == "g":
-            lo, hi = g_done * TOK // 2 // n_g, (g_done + 1) * TOK // 2 // n_g
-            core_ref[...] = lax.fori_loop(lo, hi, core_step, core_ref[...], unroll=4)
-            g_done += 1
+        if item[0] in "AG":
+            core_piece(item)
         elif item[0] == "b":
             back(*item[1:])
         elif item[1] < len(stages):
             if reduced >= 0:
                 reduce_end(reduced)
+            else:
+                core_ref[...] = jnp.concatenate([gacc[0], gacc[1]], axis=1)
             reduced = item[1]
             reduce_start(reduced)
     reduce_end(reduced)
@@ -484,7 +514,11 @@
             dqxc(h, c).wait()
             finc(h, c).wait()
             for s in range(HOPS):
-                hop(s + 1, h, c).wait_send()
+                if s == 0 and h < SPLIT:
+                    own(h, c).wait_send()
+                    rest(h, c).wait_send()
+                else:
+                    hop(s + 1, h, c).wait_send()
                 chain(s, h, c).wait_send()
 
 
@@ -495,7 +529,6 @@
 
     def step(queries, key_states, value_states, cotangent, core_aux, core_central):
         aux = jnp.transpose(core_aux, (2, 0, 1)).reshape(BOND * HQ, J1)
-        aux = jnp.pad(aux, ((0, 0), (0, JP - J1)))
         vm = pl.BlockSpec(memory_space=pltpu.VMEM)
         dma = pltpu.SemaphoreType.DMA
         pair = dma((OWN, 2))
@@ -523,8 +556,11 @@
                 pltpu.VMEM((HOPS, OWN, 2, BLK, HD), BF16),
                 pltpu.VMEM((OWN, 2, TOK, HD), BF16),
                 pltpu.VMEM((len(stages), most, JP, BOND * HQ), F32),
+                pltpu.VMEM((BOND * HQ, JP), BF16),
                 pltpu.VMEM((TOK * JP, HD), F32),
                 pltpu.VMEM((TOK * HQ, BOND * HD), BF16),
+                pltpu.VMEM((TOK * HQ // 2, BOND * HD), F32),
+                pltpu.VMEM((2, JP, BOND * HQ // 2), F32),
                 pltpu.VMEM((TOK * HQ, HD), F32),
                 pltpu.VMEM((BOND * HD, HD), BF16),
                 pltpu.VMEM((HD, BOND * HD), BF16),
@@ -541,12 +577,13 @@
                 dma((HOPS, OWN, 2)), dma((HOPS, OWN, 2)),
                 pair, pair,
                 dma((len(stages), most)), dma((len(stages), most)),
+                dma((SPLIT, 2)), dma((SPLIT, 2)),
             ],
             compiler_params=pltpu.CompilerParams(
                 collective_id=0, has_side_effects=True, vmem_limit_bytes=60 * 1024 * 1024
             ),
         )(queries[0], key_states[0], value_states[0], cotangent[0], aux, core_central)
-        core = jnp.transpose(core[:J1].reshape(J1, BOND, HQ), (2, 0, 1))
+        core = jnp.transpose(core[:J1].reshape(J1, 2, BOND, 2, OWN), (3, 1, 4, 0, 2)).reshape(HQ, J1, BOND)
         core = core / jnp.sqrt(jnp.float32(all_tokens * HD))
         return dq[None], dk[None], dv[None], core
 

time: 118 us -> 112 us (0.949); the launches traced: 116 us -> 111 us
  Pallas kernels: 109 us -> 105 us
    pallas_call x1, Pallas kernels: 109 us -> 105 us  [step(): pl.pallas_call(functools.partial(kernel, n_ctx, stages), out_shape=(jax.S...]
    unnamed x8 -> x7, local copies, waits for them, and re-layouts: 3.95 us -> 3.29 us
where the time goes in v3:
time: 112 us; the launch traced here: 111 us
  Pallas kernels  105 us (94%)
  local copies, waits for them, and re-layouts  5.42 us (5%)
    pallas_call x1, Pallas kernels, step(): pl.pallas_call(functools.partial(kernel, n_ctx, stages), out_shape=(jax.S...  105 us
    unnamed x7, local copies, waits for them, and re-layouts  3.29 us

profile of v3, /device:TPU:6, one launch (start us, length us, event | category | flops | bytes accessed | tf_op | source)
XLA Modules:
  0.0 111.5 jit_solution(13343259046397070765)
XLA Ops:
  0.6 1.4 %copy.14 = bf16[8,16,42]{2,1,0:T(8,128)(2,1)} copy(bf16[8,16,42]{2,0,1:T(8,128)(2,1)} %bitcast.23) | data formatting | bytes 21504 | tf_op jit(solution)/shard_map/transpose | solution.py:531
  2.0 104.6 %shard_map.93 = (bf16[128,2048]{1,0:T(8,128)(2,1)}, bf16[128,1024]{1,0:T(8,128)(2,1)}, bf16[128,1024]{1,0:T(8,128)(2,1)}, f32[48,128]{1,0:T(8,128)}) custom-call(bf16[128,2048]{1,0:T(8,128)(2,1)} %bitcast.15, bf16[128,1024]{1,0:T(8,128)(2,1)} %bitcast.19, bf16[128,1024]{1,0:T(8,128)(2,1)} %bitcast.20, bf16[128,5376]{1,0:T(8,128)(2,1)} %bitcast.13, ...), custom_call_target="tpu_custom_call" | custom-call | tf_op jit(solution)/shard_map/pallas_call | solution.py:537
  106.6 0.0 copy-start.1
  106.6 0.0 copy-start
  106.6 0.8 slice_multiply_fusion
  107.4 0.1 copy.15
  107.5 0.6 copy.16
  108.2 1.9 %copy.20 = bf16[1,128,2048]{2,1,0:T(8,128)(2,1)} copy(bf16[1,128,2048]{2,1,0:T(8,128)(2,1)} %bitcast.14) | data formatting | bytes 1048576
  110.1 0.0 copy-done.1
  110.1 0.7 copy.21
  110.8 0.0 copy-done
  110.8 0.7 copy.22
Async XLA Ops:
  106.6 3.5 %copy-start.1 = (bf16[128,1024]{1,0:T(8,128)(2,1)S(1)}, bf16[128,1024]{1,0:T(8,128)(2,1)}, u32[]{:S(2)}) copy-start(bf16[128,1024]{1,0:T(8,128)(2,1)} %get-tuple-element.9) | copy-start | bytes 786436
  106.6 4.1 %copy-start = (bf16[128,1024]{1,0:T(8,128)(2,1)S(1)}, bf16[128,1024]{1,0:T(8,128)(2,1)}, u32[]{:S(2)}) copy-start(bf16[128,1024]{1,0:T(8,128)(2,1)} %get-tuple-element.10) | copy-start | bytes 786436

commit v4 on v3

--- a/solution.py
+++ b/solution.py
@@ -31,39 +31,37 @@
 PIECES_G = 4
 
 FIRST = [
-    "e", "e", "e", "e", ("f", 1, 0, 0), ("f", 1, 0, 1), ("f", 1, 1, 0), ("f", 1, 1, 1), ("f", 1, 2, 0),
-    ("f", 2, 0, 0), "e", "e", ("f", 2, 0, 1), "e", ("f", 2, 1, 0), "e", "e", ("f", 3, 0, 0), "e",
-    ("f", 3, 0, 1), "e", "e", ("f", 2, 1, 1), "e", "e", "e", ("f", 4, 0, 0), "e", ("f", 4, 0, 1),
-    ("f", 3, 1, 0), "d", ("f", 3, 1, 1), ("f", 1, 2, 1),
+    "e", "e", "e", ("f", 1, 0, 0), "e", ("f", 1, 0, 1), "e", "e", ("f", 1, 1, 0), "e", ("f", 1, 1, 1), "e",
+    ("f", 2, 0, 0), "e", ("f", 2, 0, 1), "e", ("f", 2, 1, 0), "e", "e", ("f", 3, 0, 0), "e", ("f", 3, 0, 1),
+    "e", ("f", 2, 1, 1), "e", "e", ("f", 4, 0, 0), ("f", 3, 1, 0), "d", ("f", 4, 0, 1), ("f", 1, 2, 0),
+    ("f", 3, 1, 1),
 ]
 HOOKS = {
-    (0, "e"): [("f", 4, 1, 0)],
-    (0, "f"): [("b", 0, 0, 1)],
-    (0, "g"): [("f", 4, 1, 1)],
-    (0, "h"): [("b", 0, 0, 0), ("f", 2, 2, 0), ("f", 2, 2, 1), ("f", 1, 3, 0)],
-    (1, "b"): [("b", 1, 0, 1)],
-    (1, "c"): [("f", 1, 3, 1)],
+    (0, "c"): [("f", 1, 2, 1), ("f", 4, 1, 0)],
+    (0, "f"): [("f", 2, 2, 0)],
+    (0, "g"): [("b", 0, 0, 1), ("f", 4, 1, 1)],
+    (0, "h"): [("f", 2, 2, 1), ("b", 0, 0, 0), ("f", 1, 3, 0)],
+    (1, "b"): [("f", 3, 2, 0), ("b", 1, 0, 1), ("f", 1, 3, 1)],
     (1, "d"): [("b", 1, 0, 0)],
-    (1, "e"): [("f", 3, 2, 0)],
-    (1, "f"): [("b", 0, 1, 1)],
-    (1, "g"): [("b", 2, 0, 1), ("f", 3, 2, 1), ("f", 2, 3, 0)],
-    (1, "h"): [("b", 0, 1, 0), ("b", 1, 1, 1), ("f", 4, 2, 0), ("f", 2, 3, 1), ("A", 0, 0), ("b", 2, 0, 0), ("A", 0, 1), ("f", 4, 2, 1), ("G", 0, 0), ("b", 1, 1, 0), ("b", 3, 0, 1), ("G", 0, 1), ("f", 3, 3, 0)],
-    (2, "a"): [("b", 2, 1, 1)],
-    (2, "b"): [("b", 3, 0, 0), ("f", 3, 3, 1)],
-    (2, "e"): [("b", 2, 1, 0), ("f", 4, 3, 0)],
+    (1, "f"): [("b", 0, 1, 1), ("f", 3, 2, 1)],
+    (1, "g"): [("b", 2, 0, 1), ("f", 2, 3, 0), ("f", 4, 2, 0), ("A", 0, 0), ("b", 2, 0, 0)],
+    (1, "h"): [("f", 2, 3, 1), ("b", 1, 1, 1), ("f", 4, 2, 1), ("A", 0, 1), ("b", 0, 1, 0), ("G", 0, 0), ("b", 3, 0, 1), ("f", 3, 3, 0)],
+    (2, "b"): [("f", 3, 3, 1), ("b", 2, 1, 1)],
+    (2, "d"): [("b", 1, 1, 0), ("b", 3, 0, 0), ("f", 4, 3, 0)],
     (2, "f"): [("b", 0, 2, 1)],
-    (2, "g"): [("b", 3, 1, 1), ("f", 4, 3, 1)],
+    (2, "g"): [("f", 4, 3, 1), ("b", 3, 1, 1)],
     (2, "h"): [("b", 0, 2, 0)],
-    (3, "b"): [("b", 3, 1, 0), ("b", 1, 2, 1)],
+    (3, "a"): [("b", 2, 1, 0)],
+    (3, "c"): [("b", 1, 2, 1)],
     (3, "f"): [("b", 0, 3, 1)],
     (3, "g"): [("b", 1, 2, 0)],
 }
 LAST = [
-    ("b", 0, 3, 0), ("b", 2, 2, 1), ("G", 0, 2), ("G", 0, 3), ("b", 1, 3, 1), ("A", 1, 0), ("b", 4, 0, 0),
-    ("A", 1, 1), ("b", 2, 2, 0), ("G", 1, 0), ("G", 1, 1), ("b", 1, 3, 0), ("G", 1, 2), ("b", 3, 2, 1),
-    ("G", 1, 3), ("b", 2, 3, 1), ("a", 0), ("b", 2, 3, 0), ("a", 1), ("b", 3, 2, 0), ("b", 4, 2, 1),
-    ("b", 4, 0, 1), ("b", 4, 1, 0), ("b", 3, 3, 1), ("a", 2), ("b", 3, 3, 0), ("b", 4, 2, 0), ("b", 4, 1, 1),
-    ("b", 4, 3, 1), ("b", 4, 3, 0), ("a", 3),
+    ("b", 0, 3, 0), ("G", 0, 1), ("b", 2, 2, 1), ("b", 3, 1, 0), ("G", 0, 2), ("G", 0, 3), ("A", 1, 0),
+    ("b", 1, 3, 1), ("b", 1, 3, 0), ("A", 1, 1), ("G", 1, 0), ("b", 2, 2, 0), ("G", 1, 1), ("G", 1, 2),
+    ("b", 3, 2, 1), ("G", 1, 3), ("a", 0), ("b", 2, 3, 1), ("b", 2, 3, 0), ("b", 3, 2, 0), ("a", 1),
+    ("b", 4, 2, 1), ("b", 3, 3, 1), ("b", 3, 3, 0), ("a", 2), ("b", 4, 1, 1), ("b", 4, 3, 1), ("b", 4, 0, 1),
+    ("b", 4, 1, 0), ("b", 4, 2, 0), ("b", 4, 0, 0), ("b", 4, 3, 0), ("a", 3),
 ]
 
 

time: 112 us -> 111 us (level)
  no operation moved by 1% of the time
where the time goes in v4:
time: 111 us; the launch traced here: 110 us
  Pallas kernels  104 us (94%)
  local copies, waits for them, and re-layouts  5.42 us (5%)
    pallas_call x1, Pallas kernels, step(): pl.pallas_call(functools.partial(kernel, n_ctx, stages), out_shape=(jax.S...  104 us
    unnamed x7, local copies, waits for them, and re-layouts  3.29 us

profile of v4, /device:TPU:6, one launch (start us, length us, event | category | flops | bytes accessed | tf_op | source)
XLA Modules:
  0.0 110.4 jit_solution(77383251920116766)
XLA Ops:
  0.6 1.4 %copy.14 = bf16[8,16,42]{2,1,0:T(8,128)(2,1)} copy(bf16[8,16,42]{2,0,1:T(8,128)(2,1)} %bitcast.23) | data formatting | bytes 21504 | tf_op jit(solution)/shard_map/transpose | solution.py:529
  2.0 103.5 %shard_map.93 = (bf16[128,2048]{1,0:T(8,128)(2,1)}, bf16[128,1024]{1,0:T(8,128)(2,1)}, bf16[128,1024]{1,0:T(8,128)(2,1)}, f32[48,128]{1,0:T(8,128)}) custom-call(bf16[128,2048]{1,0:T(8,128)(2,1)} %bitcast.15, bf16[128,1024]{1,0:T(8,128)(2,1)} %bitcast.19, bf16[128,1024]{1,0:T(8,128)(2,1)} %bitcast.20, bf16[128,5376]{1,0:T(8,128)(2,1)} %bitcast.13, ...), custom_call_target="tpu_custom_call" | custom-call | tf_op jit(solution)/shard_map/pallas_call | solution.py:535
  105.5 0.0 copy-start.1
  105.6 0.0 copy-start
  105.6 0.8 slice_multiply_fusion
  106.4 0.1 copy.15
  106.5 0.6 copy.16
  107.1 1.9 %copy.20 = bf16[1,128,2048]{2,1,0:T(8,128)(2,1)} copy(bf16[1,128,2048]{2,1,0:T(8,128)(2,1)} %bitcast.14) | data formatting | bytes 1048576
  109.0 0.0 copy-done.1
  109.0 0.7 copy.21
  109.7 0.0 copy-done
  109.7 0.7 copy.22
Async XLA Ops:
  105.5 3.5 %copy-start.1 = (bf16[128,1024]{1,0:T(8,128)(2,1)S(1)}, bf16[128,1024]{1,0:T(8,128)(2,1)}, u32[]{:S(2)}) copy-start(bf16[128,1024]{1,0:T(8,128)(2,1)} %get-tuple-element.9) | copy-start | bytes 786436
  105.6 4.1 %copy-start = (bf16[128,1024]{1,0:T(8,128)(2,1)S(1)}, bf16[128,1024]{1,0:T(8,128)(2,1)}, u32[]{:S(2)}) copy-start(bf16[128,1024]{1,0:T(8,128)(2,1)} %get-tuple-element.10) | copy-start | bytes 786436
